TPU v7x, 32 devices: a whole 2x2x4 slice. The times are simulated.
32 devices in a mesh: group: 8 (over z, y), mp: 4 (over x, core).
Axes of the slice: x: 2, y: 2, z: 4, core: 2. Of those that a mesh axis runs over, the one named last changes fastest.
Arguments:
- observations: bfloat16 [1024, 512], P('group', 'mp'), may hold values from -6 to 6
- hidden_state: bfloat16 [512, 1024], P('group', 'mp'), may hold values from -0.8984375 to 0.8984375
- cell_state: bfloat16 [512, 1024], P('group', 'mp'), may hold values from -4 to 4
- arrival_order: int32 [512], replicated, may hold values from 0 to 511, as said below
- batch_counts: int32 [8], replicated, may hold values from 0 to 128, as said below
- input_weight: bfloat16 [512, 4, 1024], P(None, None, 'mp'), may hold values from -0.15625 to 0.15625
- state_weight: bfloat16 [1024, 4, 1024], P(None, None, 'mp'), may hold values from -0.15625 to 0.15625
- gate_bias: float32 [4, 1024], P(None, 'mp'), may hold values from -3 to 3
- head_weight: bfloat16 [1024, 2, 512], P(None, None, 'mp'), may hold values from -0.1875 to 0.1875
- head_bias: float32 [2, 512], P(None, 'mp'), may hold values from -3 to 3
- value_weight: bfloat16 [512, 1], P('mp'), may hold values from -0.25 to 0.25
- value_bias: float32 [1], replicated, may hold values from -3 to 3
- advantage_weight: bfloat16 [512, 18], P('mp'), may hold values from -0.25 to 0.25
- advantage_bias: float32 [18], replicated, may hold values from -3 to 3
Outputs:
- action_values: float32 [1024, 18], P('group')
- new_hidden: bfloat16 [512, 1024], P('group', 'mp')
- new_cell: bfloat16 [512, 1024], P('group', 'mp')
Inputs may be any that keep to these rules, and one draw needn't show every extreme that they name: `arrival_order`: A permutation: each actor id once. Positions starts[b] to starts[b] + batch_counts[b] - 1 hold the actors of batch b, where starts is the running sum of batch_counts. Of the actors of one owner (ids k * 64 to (k + 1) * 64 - 1), at most 16 lie in one batch. `batch_counts`: sums to 512.
All inputs are finite; a program needn't handle non-finite values.
Results may differ from a plain program's by a relative error of at most 0.0019.
Values may be sent and summed in bfloat16 or wider, within the bound.
No kernel may reach another device: no remote copies, remote signals or barrier semaphores. Data moves between devices by JAX's collectives and lax.ppermute only.
A program may use at most 64 MiB of HBM per device.

v0:
```python
import math

import jax
import jax.numpy as jnp
from jax import lax
from jax.sharding import PartitionSpec as P


def with_blank(table):
    blank = jnp.zeros((1,) + table.shape[1:], table.dtype)
    return jnp.concatenate([table, blank], axis=0)


def invert_slots(slot_of, capacity, missing):
    slots = jnp.arange(capacity, dtype=jnp.int32)
    items = jnp.arange(slot_of.shape[0], dtype=jnp.int32)
    hits = slot_of[None, :] == slots[:, None]
    found = jnp.any(hits, axis=1)
    picked = jnp.sum(jnp.where(hits, items[None, :], 0), axis=1)
    return jnp.where(found, picked, missing)


def owned_positions(arrival_order, own_index, per_owner):
    actor_total = arrival_order.shape[0]
    block_len = math.gcd(actor_total, 2048)
    block_count = actor_total // block_len
    local_ids = (arrival_order - own_index * per_owner).reshape(block_count, block_len)
    bases = jnp.arange(block_count, dtype=jnp.int32) * block_len
    owned = jnp.arange(per_owner, dtype=jnp.int32)
    offsets = jnp.arange(block_len, dtype=jnp.int32)

    def accumulate(total, pair):
        ids, base = pair
        hits = ids[None, :] == owned[:, None]
        found = jnp.sum(jnp.where(hits, (base + offsets)[None, :], 0), axis=1)
        return (total + found, None)

    result, _ = lax.scan(accumulate, jnp.zeros((per_owner,), jnp.int32), (local_ids, bases))
    return result


def advance(
    obs_part,
    hidden_part,
    cell_part,
    input_weight,
    state_weight,
    gate_bias,
    head_weight,
    head_bias,
    value_weight,
    value_bias,
    advantage_weight,
    advantage_bias,
):
    full_obs, full_hidden = (
        lax.all_gather(obs_part, "mp", axis=1, tiled=True),
        lax.all_gather(hidden_part, "mp", axis=1, tiled=True),
    )
    row_count = obs_part.shape[0]
    unit_count = cell_part.shape[1]
    gate_values = jnp.dot(
        full_obs,
        input_weight.reshape(input_weight.shape[0], -1),
        preferred_element_type=jnp.float32,
    )
    gate_values = gate_values + jnp.dot(
        full_hidden,
        state_weight.reshape(state_weight.shape[0], -1),
        preferred_element_type=jnp.float32,
    )
    gate_values = gate_values.reshape(row_count, 4, unit_count) + gate_bias[None]
    cell_next = jax.nn.sigmoid(gate_values[:, 1]) * cell_part.astype(jnp.float32) + jax.nn.sigmoid(
        gate_values[:, 0]
    ) * jnp.tanh(gate_values[:, 2])
    hidden_next = (jax.nn.sigmoid(gate_values[:, 3]) * jnp.tanh(cell_next)).astype(jnp.bfloat16)
    whole_next = lax.all_gather(hidden_next, "mp", axis=1, tiled=True)
    head_units = head_weight.shape[2]
    stream = jnp.dot(
        whole_next,
        head_weight.reshape(head_weight.shape[0], -1),
        preferred_element_type=jnp.float32,
    )
    stream = jax.nn.relu(stream.reshape(row_count, 2, head_units) + head_bias[None]).astype(
        jnp.bfloat16
    )
    value_part = jnp.dot(stream[:, 0], value_weight, preferred_element_type=jnp.float32)
    advantage_part = jnp.dot(stream[:, 1], advantage_weight, preferred_element_type=jnp.float32)
    value_sum, advantage_sum = lax.psum((value_part, advantage_part), "mp")
    value_sum = value_sum + value_bias
    advantage_sum = advantage_sum + advantage_bias
    slot_values = value_sum + advantage_sum - jnp.mean(advantage_sum, axis=1, keepdims=True)
    return (hidden_next, cell_next.astype(jnp.bfloat16), slot_values)


def per_device(
    observations,
    hidden_state,
    cell_state,
    arrival_order,
    batch_counts,
    input_weight,
    state_weight,
    gate_bias,
    head_weight,
    head_bias,
    value_weight,
    value_bias,
    advantage_weight,
    advantage_bias,
):
    batch_total = batch_counts.shape[0]
    per_owner = hidden_state.shape[0]
    capacity = observations.shape[0]
    per_pair = capacity // batch_total
    own_index = lax.axis_index("group")
    batch_ends = jnp.cumsum(batch_counts)
    batch_starts = batch_ends - batch_counts
    own_positions = owned_positions(arrival_order, own_index, per_owner)
    own_batch = jnp.sum((own_positions[:, None] >= batch_ends[None, :]).astype(jnp.int32), axis=1)
    earlier = (own_batch[:, None] == own_batch[None, :]) & (
        own_positions[None, :] < own_positions[:, None]
    )
    own_rank = jnp.sum(earlier.astype(jnp.int32), axis=1)
    send_slot = own_batch * per_pair + own_rank
    send_index = invert_slots(send_slot, capacity, per_owner)
    local_slot = jnp.arange(capacity, dtype=jnp.int32)
    own_count = batch_counts[own_index]
    own_start = batch_starts[own_index]
    filled = local_slot < own_count
    slot_actor = lax.dynamic_slice_in_dim(
        jnp.concatenate([arrival_order, jnp.zeros((capacity,), jnp.int32)]), own_start, capacity
    )
    slot_owner = jnp.where(filled, slot_actor // per_owner, batch_total)
    before = (slot_owner[:, None] == slot_owner[None, :]) & (
        local_slot[None, :] < local_slot[:, None]
    )
    slot_rank = jnp.sum(before.astype(jnp.int32), axis=1)
    recv_slot = jnp.where(filled, slot_owner * per_pair + slot_rank, capacity)
    return_index = invert_slots(recv_slot, capacity, capacity)
    feature_count = observations.shape[1]
    obs_send = with_blank(observations)[return_index].reshape(batch_total, per_pair, feature_count)
    obs_got = lax.all_to_all(obs_send, "group", split_axis=0, concat_axis=0, tiled=True)
    obs_rows = obs_got.reshape(capacity, feature_count)[send_slot]
    new_hidden, new_cell, owner_values = advance(
        obs_rows,
        hidden_state,
        cell_state,
        input_weight,
        state_weight,
        gate_bias,
        head_weight,
        head_bias,
        value_weight,
        value_bias,
        advantage_weight,
        advantage_bias,
    )
    action_count = owner_values.shape[1]
    values_send = with_blank(owner_values)[send_index].reshape(batch_total, per_pair, action_count)
    values_got = lax.all_to_all(values_send, "group", split_axis=0, concat_axis=0, tiled=True)
    action_values = with_blank(values_got.reshape(capacity, action_count))[recv_slot]
    return (action_values, new_hidden, new_cell)


def solution(mesh):
    placed = (
        P("group", "mp"),
        P("group", "mp"),
        P("group", "mp"),
        P(),
        P(),
        P(None, None, "mp"),
        P(None, None, "mp"),
        P(None, "mp"),
        P(None, None, "mp"),
        P(None, "mp"),
        P("mp", None),
        P(),
        P("mp", None),
        P(),
    )
    return jax.shard_map(
        per_device,
        mesh=mesh,
        in_specs=placed,
        out_specs=(P("group", None), P("group", "mp"), P("group", "mp")),
        check_vma=False,
    )
```

profile of v0, /device:TPU:0, one launch (start us, length us, event | category | flops | bytes accessed | tf_op | source)
XLA Modules:
  0.0 73.3 jit_solution(15401646834344015845)
XLA Ops:
  0.6 0.0 copy-start
  0.6 0.8 %reduce-window.8 = s32[8,1]{0,1:T(1,128)S(1)} reduce-window(s32[8,1]{0,1:T(1,128)} %bitcast.89, s32[]{:T(128)} %constant.24.clone.1), window={size=8x1 pad=7_0x0_0}, to_apply=%region_0.0 | reduce-window | flops 56 | bytes 68 | tf_op jit(solution)/shard_map/reduce-window.3
  1.5 0.7 bitcast_subtract_fusion
  2.1 1.2 %dynamic_slice.15 = s32[1]{0:T(128)} dynamic-slice(s32[8]{0:T(128)} %param.18, s32[]{:T(128)S(6)} %select_n.91), dynamic_slice_sizes={1} | dynamic-slice | bytes 12 | tf_op jit(solution)/shard_map/dynamic_slice | solution.py:128
  3.4 0.6 dynamic_slice.16
  5.9 1.4 %compare_select_fusion.8 = s32[128]{0:T(128)S(1)} fusion(s32[]{:T(128)S(6)} %select_n.92, s32[512]{0:T(512)} %param.17, s32[]{:T(128)} %bitcast), kind=kLoop, calls=%fused_computation.65 | loop fusion | flops 2176 | bytes 2568 | tf_op jit(solution)/shard_map/jit(_where)/select_n | solution.py:134
  7.3 0.2 convert_reduce_fusion
  7.5 1.4 %compare_select_fusion = (s32[128]{0:T(128)S(1)}, s32[128]{0:T(128)S(1)}) fusion(s32[128]{0:T(128)S(1)} %convert_reduce_fusion, s32[]{:T(128)} %bitcast, s32[]{:T(128)S(6)} %select_n.92, s32[512]{0:T(512)} %param.17), kind=kLoop, calls=%fused_computation.56 | loop fusion | flops 2944 | bytes 3592 | tf_op jit(solution)/shard_map/select_n | solution.py:162
  8.9 0.1 fusion.19
  9.0 0.1 select_reduce_fusion.1
  9.2 0.8 %concatenate.12 = bf16[129,128]{1,0:T(8,128)(2,1)S(1)} pad(bf16[128,128]{1,0:T(8,128)(2,1)} %param.14, bf16[]{:T(256)} %constant.20.clone.1), padding=0_1x0_0 | pad | bytes 65794 | tf_op jit(solution)/shard_map/concatenate | solution.py:11
  9.9 1.3 %gather_fusion = bf16[128,128]{1,0:T(8,128)(2,1)} fusion(bf16[129,128]{1,0:T(8,128)(2,1)S(1)} %concatenate.12, s32[1024]{0:T(1024)S(1)} %pad_clamp_fusion.3), kind=kCustom, calls=%fused_computation | custom fusion | bytes 66048 | tf_op jit(solution)/shard_map/gather | solution.py:142
  11.3 7.3 %all-to-all-start = ((bf16[8,16,128]{2,1,0:T(8,128)(2,1)}), bf16[8,16,128]{2,1,0:T(8,128)(2,1)S(1)}, u32[]{:S(2)}, u32[]{:S(2)}) async-start(bf16[8,16,128]{2,1,0:T(8,128)(2,1)} %bitcast.6), calls=%async_computation | async-start | bytes 65536 | tf_op jit(solution)/shard_map/all_to_all | solution.py:143
  18.6 0.8 %broadcast_subtract_fusion = s32[512]{0:T(512)S(1)} fusion(s32[512]{0:T(512)} %param.17, s32[]{:T(128)S(6)} %mul.38), kind=kLoop, calls=%fused_computation.66 | loop fusion | flops 512 | bytes 4100 | tf_op jit(solution)/shard_map/sub | solution.py:27
  19.4 0.1 select_reduce_fusion
  19.5 0.1 convert_reduce_fusion.2
  19.6 0.2 convert_reduce_fusion.1
  19.8 0.1 fusion.22
  19.9 0.1 select_reduce_fusion.2
  20.0 1.4 %copy.27 = bf16[64,8,4,256]{3,1,2,0:T(8,128)(2,1)S(1)} copy(bf16[64,8,4,256]{3,2,1,0:T(4,128)(2,1)} %bitcast.83) | data formatting | bytes 2097152
  21.5 0.0 copy-start.3
  21.5 0.5 copy.28
  22.0 0.5 copy-done.3
  22.5 0.9 %copy.32 = bf16[128,8,2,128]{3,1,2,0:T(8,128)(2,1)} copy(bf16[128,8,2,128]{3,2,1,0:T(2,128)(2,1)S(1)} %bitcast.86) | data formatting | bytes 1048576
  23.4 2.1 %copy.22 = bf16[256,1024]{1,0:T(8,128)(2,1)} copy(bf16[256,1024]{0,1:T(8,128)(2,1)} %bitcast.82) | data formatting | bytes 1048576 | tf_op jit(solution)/shard_map/dot_general | solution.py:79
  26.1 5.4 %all_gather.10 = bf16[64,1024]{1,0:T(8,128)(2,1)S(1)} all-gather(bf16[64,256]{1,0:T(8,128)(2,1)S(1)} %copy-done.5), channel_id=1, replica_groups=mesh['group'=8,'mp'=4] {'mp'}, dimensions={1}, use_global_device_ids=true | all-gather | bytes 163840 | tf_op jit(solution)/shard_map/all_gather | solution.py:58
  31.6 0.6 gather_fusion.1
  32.2 5.3 %all-gather = bf16[64,512]{1,0:T(8,128)(2,1)S(1)} all-gather(bf16[64,128]{1,0:T(8,128)(2,1)S(1)} %gather_fusion.1), channel_id=2, replica_groups=mesh['group'=8,'mp'=4] {'mp'}, dimensions={1}, use_global_device_ids=true | all-gather | bytes 81920 | tf_op jit(solution)/shard_map/all_gather | solution.py:57
  37.5 0.3 fusion.29
  37.8 0.5 convolution_add_fusion
  38.4 0.7 fusion.27
  39.1 5.4 %all_gather.11 = bf16[64,1024]{1,0:T(8,128)(2,1)S(1)} all-gather(bf16[64,256]{1,0:T(8,128)(2,1)S(1)} %fusion.20), channel_id=1, replica_groups=mesh['group'=8,'mp'=4] {'mp'}, dimensions={1}, use_global_device_ids=true | all-gather | bytes 163840 | tf_op jit(solution)/shard_map/all_gather | solution.py:77
  44.5 0.3 fusion.1
  44.8 0.1 fusion.23
  44.9 0.1 convolution_bitcast_fusion
  45.1 11.4 %all-reduce.4 = (f32[64,18]{0,1:T(8,128)S(1)}, f32[64,1]{0,1:T(1,128)S(1)}) all-reduce(f32[64,18]{0,1:T(8,128)S(1)} %fusion.23, f32[64,1]{0,1:T(1,128)S(1)} %convolution_bitcast_fusion), channel_id=1, replica_groups=mesh['group'=8,'mp'=4] {'mp'}, use_global_device_ids=true, to_apply=%region_8.9 | all-reduce | flops 1216 | bytes 9728 | tf_op jit(solution)/shard_map/psum | solution.py:89
  56.5 0.1 add_reduce_fusion
  56.6 0.1 add_subtract_fusion
  56.7 0.1 copy.25
  56.8 0.6 gather_fusion.2
  57.4 0.7 reshape.224
  58.1 6.0 %all-to-all-start.1 = ((f32[8,1,288]{2,1,0:T(1,128)}), f32[8,1,288]{2,1,0:T(1,128)S(1)}, u32[]{:S(2)}, u32[]{:S(2)}) async-start(f32[8,1,288]{2,1,0:T(1,128)} %reshape.224), calls=%async_computation.1 | async-start | bytes 24576 | tf_op jit(solution)/shard_map/all_to_all | solution.py:161
  64.1 6.5 %all-to-all-done.1 = f32[8,1,288]{2,1,0:T(1,128)S(1)} async-done(((f32[8,1,288]{2,1,0:T(1,128)}), f32[8,1,288]{2,1,0:T(1,128)S(1)}, u32[]{:S(2)}, u32[]{:S(2)}) %all-to-all-start.1) | async-done | bytes 9248 | tf_op jit(solution)/shard_map/all_to_all | solution.py:161
  70.7 0.5 broadcast.164
  71.2 0.7 reduce
  71.9 0.1 reshape.225
  72.0 0.6 gather_fusion.3
  72.6 0.7 copy.24
  (33 shorter events, 0.2 us)
Async XLA Ops:
  0.6 44.2 %copy-start = (bf16[128,18]{0,1:T(8,128)(2,1)S(1)}, bf16[128,18]{0,1:T(8,128)(2,1)}, u32[]{:S(2)}) copy-start(bf16[128,18]{0,1:T(8,128)(2,1)} %param.26) | copy-start | bytes 13828
  11.3 20.3 %all-to-all-start = ((bf16[8,16,128]{2,1,0:T(8,128)(2,1)}), bf16[8,16,128]{2,1,0:T(8,128)(2,1)S(1)}, u32[]{:S(2)}, u32[]{:S(2)}) async-start(bf16[8,16,128]{2,1,0:T(8,128)(2,1)} %bitcast.6), calls=%async_computation | async-start | bytes 65536 | tf_op jit(solution)/shard_map/all_to_all | solution.py:143
  18.6 2.9 %copy-start.1 = (bf16[1024,4,256]{2,1,0:T(4,128)(2,1)S(1)}, bf16[1024,4,256]{2,1,0:T(4,128)(2,1)}, u32[]{:S(2)}) copy-start(bf16[1024,4,256]{2,1,0:T(4,128)(2,1)} %param.20) | copy-start | bytes 6291460
  21.5 1.0 %copy-start.3 = (bf16[1024,2,128]{2,1,0:T(2,128)(2,1)S(1)}, bf16[1024,2,128]{2,1,0:T(2,128)(2,1)}, u32[]{:S(2)}) copy-start(bf16[1024,2,128]{2,1,0:T(2,128)(2,1)} %param.22) | copy-start | bytes 1572868
  22.0 4.1 %copy-start.5 = (bf16[64,256]{1,0:T(8,128)(2,1)S(1)}, bf16[64,256]{1,0:T(8,128)(2,1)}, u32[]{:S(2)}) copy-start(bf16[64,256]{1,0:T(8,128)(2,1)} %param.15) | copy-start | bytes 98308
  32.2 6.1 %copy-start.7 = (f32[4,256]{1,0:T(4,128)S(1)}, f32[4,256]{1,0:T(4,128)}, u32[]{:S(2)}) copy-start(f32[4,256]{1,0:T(4,128)} %param.21) | copy-start | bytes 12292
  37.5 0.9 %copy-start.6 = (bf16[64,256]{1,0:T(8,128)(2,1)S(1)}, bf16[64,256]{1,0:T(8,128)(2,1)}, u32[]{:S(2)}) copy-start(bf16[64,256]{1,0:T(8,128)(2,1)} %param.16) | copy-start | bytes 98308
  37.8 6.7 %copy-start.2 = (bf16[256,1024]{1,0:T(8,128)(2,1)S(1)}, bf16[256,1024]{1,0:T(8,128)(2,1)}, u32[]{:S(2)}) copy-start(bf16[256,1024]{1,0:T(8,128)(2,1)} %copy.22) | copy-start | bytes 1572868
  37.8 6.7 %copy-start.9 = (f32[2,128]{1,0:T(2,128)S(1)}, f32[2,128]{1,0:T(2,128)}, u32[]{:S(2)}) copy-start(f32[2,128]{1,0:T(2,128)} %param.23) | copy-start | bytes 3076
  37.8 7.1 %copy-start.10 = (bf16[128,1]{0,1:T(2,128)(2,1)S(1)}, bf16[128,1]{0,1:T(2,128)(2,1)}, u32[]{:S(2)}) copy-start(bf16[128,1]{0,1:T(2,128)(2,1)} %param.24) | copy-start | bytes 772
  37.8 18.7 %copy-start.8 = (f32[18]{0:T(128)S(1)}, f32[18]{0:T(128)}, u32[]{:S(2)}) copy-start(f32[18]{0:T(128)} %param.27) | copy-start | bytes 220
  39.1 34.2 %copy-start.4 = (bf16[64,256]{1,0:T(8,128)(2,1)}, bf16[64,256]{1,0:T(8,128)(2,1)S(1)}, u32[]{:S(2)}) copy-start(bf16[64,256]{1,0:T(8,128)(2,1)S(1)} %fusion.20) | copy-start | bytes 98308
  58.1 12.5 %all-to-all-start.1 = ((f32[8,1,288]{2,1,0:T(1,128)}), f32[8,1,288]{2,1,0:T(1,128)S(1)}, u32[]{:S(2)}, u32[]{:S(2)}) async-start(f32[8,1,288]{2,1,0:T(1,128)} %reshape.224), calls=%async_computation.1 | async-start | bytes 24576 | tf_op jit(solution)/shard_map/all_to_all | solution.py:161
where the time goes:
time: 74 us; the launch traced here: 73.3 us
  blocking collectives  27.5 us (37%)
  local copies, waits for them, and re-layouts  13.4 us (18%)
  starting transfers between devices  13.3 us (18%)
  other arithmetic  7.76 us (10%)
  waiting for transfers between devices  6.54 us (9%)
  between operations  3.48 us (5%)
  matrix products  1.32 us (2%)
    psum x1, blocking collectives, advance(): value_sum, advantage_sum = lax.psum((value_part, advantage_part), 'mp')  11.4 us
    all_to_all x1, starting transfers between devices, per_device(): lax.all_to_all(obs_send, 'group', split_axis=0, concat_axis=0, tiled=True)  7.31 us
    all_to_all x1, waiting for transfers between devices, per_device(): lax.all_to_all(values_send, 'group', split_axis=0, concat_axis=0, tiled=T...  6.54 us
    all_to_all x1, starting transfers between devices, per_device(): lax.all_to_all(values_send, 'group', split_axis=0, concat_axis=0, tiled=T...  5.99 us
    all_gather x1, blocking collectives, advance(): lax.all_gather(hidden_part, 'mp', axis=1, tiled=True)  5.42 us
    all_gather x1, blocking collectives, advance(): whole_next = lax.all_gather(hidden_next, 'mp', axis=1, tiled=True)  5.42 us
    all_gather x1, blocking collectives, advance(): lax.all_gather(obs_part, 'mp', axis=1, tiled=True)  5.27 us
    unnamed x29, local copies, waits for them, and re-layouts  4.95 us
  transfers between devices with their start and end apart: 2, of which 1 were waited for; matrix products, arithmetic and copies ran while one was open for 9% of the time, Pallas kernels for 0%

commit v1 on v0

v1 whole, which is shorter than its diff:
```python
import functools

import jax
import jax.numpy as jnp
from jax import lax
from jax.experimental import pallas as pl
from jax.experimental.pallas import tpu as pltpu
from jax.sharding import PartitionSpec as P

BF16 = jnp.bfloat16
F32 = jnp.float32
I32 = jnp.int32
EXACT = lax.Precision.HIGHEST
VMEM = pl.BlockSpec(memory_space=pltpu.VMEM)
SMEM = pl.BlockSpec(memory_space=pltpu.SMEM)


def iota(shape, axis):
    return lax.broadcasted_iota(I32, shape, axis)


def split(values, divisor):
    if divisor & (divisor - 1) == 0:
        quotient = lax.shift_right_logical(values, jnp.int32(divisor.bit_length() - 1))
    else:
        quotient = ((values.astype(F32) + 0.5) * (1.0 / divisor)).astype(I32)
    return quotient, values - quotient * divisor


def one_hot(mask):
    return jnp.where(mask, 1.0, 0.0).astype(BF16)


def dot(left, right, contract=((1,), (0,)), precision=None):
    return lax.dot_general(
        left, right, (contract, ((), ())), precision=precision, preferred_element_type=F32
    )


def route_kernel(mp, per_owner, counts_ref, order_ref, obs_ref, send_ref, base_ref, slot_ref):
    blocks, capacity = order_ref.shape
    batches = counts_ref.shape[0]
    per_pair = capacity // batches
    own = lax.axis_index("group")
    ends = []
    total = jnp.int32(0)
    start = jnp.int32(0)
    for batch in range(batches):
        start = jnp.where(own == batch, total, start)
        total = total + counts_ref[batch]
        ends.append(total)
    count = counts_ref[own]
    lanes = iota((1, capacity), 1)
    batch_ids = iota((batches, capacity), 0)
    earlier = one_hot(iota((capacity, capacity), 0) < iota((capacity, capacity), 1))

    block, shift = split(start, capacity)
    first = order_ref[pl.ds(jnp.minimum(block, blocks - 1), 1), :]
    second = order_ref[pl.ds(jnp.minimum(block + 1, blocks - 1), 1), :]
    turn = lax.rem(capacity - shift, capacity)
    merged = jnp.where(lanes >= shift, first, second)
    window = pltpu.roll(jnp.broadcast_to(merged, (8, capacity)), turn, 1)[0:1]
    owner, _ = split(window, per_owner)
    filled = lanes < count
    by_owner = one_hot((batch_ids == owner) & filled)
    ahead = dot(by_owner, earlier)
    rank = jnp.sum(by_owner.astype(F32) * ahead, axis=0, keepdims=True).astype(I32)
    row_ids, rank_ids = split(iota((mp * capacity, capacity), 0), per_pair)
    row_owner, _ = split(row_ids, mp)
    target = jnp.where(filled, owner * per_pair + rank, -1)
    send_ref[...] = dot(
        one_hot(row_owner * per_pair + rank_ids == target), obs_ref[...]
    ).astype(send_ref.dtype)
    slot_ref[0:1, :] = jnp.where(filled, owner, -1)
    slot_ref[1:2, :] = rank

    actors = iota((per_owner, capacity), 0) + own * per_owner
    carry = jnp.zeros((batches, 1), F32)
    base = jnp.zeros((per_owner, 1), F32)
    for index in range(blocks):
        ids = order_ref[index : index + 1, :]
        here = lanes + index * capacity
        batch = jnp.zeros((1, capacity), I32)
        for end in ends:
            batch = batch + jnp.where(here >= end, 1, 0)
        mine = (ids >= own * per_owner) & (ids < (own + 1) * per_owner)
        by_batch = one_hot((batch_ids == batch) & mine)
        ahead = dot(by_batch, earlier) + carry
        wide = by_batch.astype(F32)
        place = jnp.sum(wide * ahead, axis=0, keepdims=True)
        place = place + (batch * (mp * per_pair)).astype(F32)
        carry = carry + jnp.sum(wide, axis=1, keepdims=True)
        base = base + jnp.sum(jnp.where(ids == actors, place, 0.0), axis=1, keepdims=True)
    base_ref[...] = jnp.broadcast_to(base, base_ref.shape).astype(I32)


def cell_kernel(
    mp, per_pair, offsets, base_ref, rows_ref, hidden_refs, cell_ref, input_ref, state_ref, bias_ref,
    hidden_ref, next_ref,
):
    per_owner, units = cell_ref.shape
    features = rows_ref.shape[1]
    me = lax.axis_index("mp")
    base = base_ref[:, 0:1]
    columns = iota((per_owner, rows_ref.shape[0]), 1)
    picks = jnp.concatenate([one_hot(columns == base + part * per_pair) for part in range(mp)], axis=0)
    picked = dot(picks, rows_ref[...]).astype(BF16)
    gates = None
    for part in range(mp):
        term = dot(
            picked[part * per_owner : (part + 1) * per_owner],
            input_ref[part * features : (part + 1) * features, :],
        )
        gates = term if gates is None else gates + term
    for (ref, column), offset in zip(hidden_refs, offsets):
        rows = pl.ds(pl.multiple_of(jnp.bitwise_xor(me, offset) * units, units), units)
        gates = gates + dot(ref[:, column : column + units], state_ref[rows, :])
    gate = [
        gates[:, k * units : (k + 1) * units] + bias_ref[k : k + 1, :] for k in range(4)
    ]
    cell = jax.nn.sigmoid(gate[1]) * cell_ref[...].astype(F32) + jax.nn.sigmoid(gate[0]) * jnp.tanh(gate[2])
    next_ref[...] = cell.astype(BF16)
    hidden_ref[...] = (jax.nn.sigmoid(gate[3]) * jnp.tanh(cell)).astype(BF16)


def head_kernel(
    mp, per_pair, offsets, base_ref, hidden_refs, head_ref, head_bias_ref, value_ref, value_bias_ref,
    advantage_ref, advantage_bias_ref, send_ref,
):
    per_owner = base_ref.shape[0]
    units = head_ref.shape[0] // mp
    width = head_bias_ref.shape[1]
    actions = advantage_ref.shape[0]
    me = lax.axis_index("mp")
    total = None
    for (ref, column), offset in zip(hidden_refs, offsets):
        rows = pl.ds(pl.multiple_of(jnp.bitwise_xor(me, offset) * units, units), units)
        term = dot(ref[:, column : column + units], head_ref[rows, :])
        total = term if total is None else total + term
    value_stream = jnp.maximum(total[:, :width] + head_bias_ref[0:1, :], 0.0).astype(BF16)
    advantage_stream = jnp.maximum(total[:, width:] + head_bias_ref[1:2, :], 0.0).astype(BF16)
    value = jnp.sum(
        value_stream.astype(F32) * value_ref[...].astype(F32), axis=1, keepdims=True
    )
    advantage = dot(advantage_stream, advantage_ref[...], ((1,), (1,)))
    first = jnp.where(me == 0, 1.0, 0.0)
    advantage = advantage + advantage_bias_ref[...] * first
    value = value + value_bias_ref[0] * first
    mixed = value + advantage - jnp.sum(advantage, axis=1, keepdims=True) * (1.0 / actions)
    lanes = send_ref.shape[2]
    lane_rank, lane_action = split(iota((actions, lanes), 1), actions)
    spread = dot(
        mixed,
        jnp.where(
            (lane_action == iota((actions, lanes), 0)) & (lane_rank < per_pair), 1.0, 0.0
        ),
        precision=EXACT,
    )
    batch, rank = split(base_ref[:, 0:1], mp * per_pair)
    spread = jnp.where(split(iota((per_owner, lanes), 1), actions)[0] == rank, spread, 0.0)
    rows = send_ref.shape[0]
    to_row = jnp.where(split(iota((per_owner, rows), 1), mp)[0] == batch, 1.0, 0.0)
    send_ref[:, 0, :] = dot(to_row, spread, ((0,), (0,)), precision=EXACT)


def place_kernel(mp, per_pair, slot_ref, rows_ref, out_ref):
    actions, capacity = out_ref.shape
    rows, _, lanes = rows_ref.shape
    owner = slot_ref[0:1, :]
    rank = slot_ref[1:2, :]
    to_slot = jnp.where(split(iota((rows, capacity), 0), mp)[0] == owner, 1.0, 0.0)
    spread = dot(rows_ref[:, 0, :], to_slot, ((0,), (0,)), precision=EXACT)
    spread = jnp.where(split(iota((lanes, capacity), 0), actions)[0] == rank, spread, 0.0)
    lane_rank, lane_action = split(iota((actions, lanes), 1), actions)
    pick = jnp.where((lane_action == iota((actions, lanes), 0)) & (lane_rank < per_pair), 1.0, 0.0)
    out_ref[...] = dot(pick, spread, precision=EXACT)


def call(kernel, out_shape, specs, *args):
    return pl.pallas_call(
        kernel,
        out_shape=out_shape,
        in_specs=specs,
        out_specs=jax.tree.map(lambda _: VMEM, out_shape),
    )(*args)


def gather_parts(part, mp):
    arrays = [part]
    places = [(0, 0)]
    offsets = [0]
    width = part.shape[1]
    current = part
    distance = mp // 2
    while distance:
        pairs = [(device, device ^ distance) for device in range(mp)]
        got = lax.ppermute(current, "mp", pairs)
        places += [(len(arrays), k * width) for k in range(got.shape[1] // width)]
        arrays.append(got)
        offsets += [offset ^ distance for offset in offsets]
        distance //= 2
        if distance:
            current = jnp.concatenate([current, got], axis=1)
    return arrays, places, offsets


def per_device(
    observations,
    hidden_state,
    cell_state,
    arrival_order,
    batch_counts,
    input_weight,
    state_weight,
    gate_bias,
    head_weight,
    head_bias,
    value_weight,
    value_bias,
    advantage_weight,
    advantage_bias,
    *,
    mp,
):
    batches = batch_counts.shape[0]
    capacity, features = observations.shape
    per_owner, units = cell_state.shape
    per_pair = capacity // batches
    actions = advantage_weight.shape[1]
    rows = batches * mp
    everyone = ("group", "mp")

    hidden_arrays, hidden_places, offsets = gather_parts(hidden_state, mp)
    send, base, slot = call(
        functools.partial(route_kernel, mp, per_owner),
        (
            jax.ShapeDtypeStruct((rows * per_pair, features), BF16),
            jax.ShapeDtypeStruct((per_owner, 128), I32),
            jax.ShapeDtypeStruct((2, capacity), I32),
        ),
        [SMEM, VMEM, VMEM],
        batch_counts,
        arrival_order.reshape(-1, capacity),
        observations,
    )
    got = lax.all_to_all(send, everyone, 0, 0, tiled=True)

    count = len(hidden_arrays)

    def cell_body(base_ref, rows_ref, *refs):
        places = [(refs[array], column) for array, column in hidden_places]
        cell_kernel(mp, per_pair, offsets, base_ref, rows_ref, places, *refs[count:])

    new_hidden, new_cell = call(
        cell_body,
        (
            jax.ShapeDtypeStruct((per_owner, units), BF16),
            jax.ShapeDtypeStruct((per_owner, units), BF16),
        ),
        [VMEM] * (6 + count),
        base,
        got,
        *hidden_arrays,
        cell_state,
        input_weight.reshape(input_weight.shape[0], -1),
        state_weight.reshape(state_weight.shape[0], -1),
        gate_bias,
    )

    next_arrays, next_places, _ = gather_parts(new_hidden, mp)

    def head_body(base_ref, *refs):
        places = [(refs[array], column) for array, column in next_places]
        head_kernel(mp, per_pair, offsets, base_ref, places, *refs[count:])

    lanes = -(-per_pair * actions // 128) * 128
    values = call(
        head_body,
        jax.ShapeDtypeStruct((rows, 1, lanes), F32),
        [VMEM] * (4 + count) + [SMEM, VMEM, VMEM],
        base,
        *next_arrays,
        head_weight.reshape(head_weight.shape[0], -1),
        head_bias,
        value_weight.T,
        value_bias,
        advantage_weight.T,
        advantage_bias.reshape(1, -1),
    )
    back = lax.all_to_all(values, everyone, 0, 0, tiled=True)
    placed = call(
        functools.partial(place_kernel, mp, per_pair),
        jax.ShapeDtypeStruct((actions, capacity), F32),
        [VMEM, VMEM],
        slot,
        back,
    )
    return placed.T, new_hidden, new_cell


def solution(mesh):
    placed = (
        P("group", "mp"),
        P("group", "mp"),
        P("group", "mp"),
        P(),
        P(),
        P(None, None, "mp"),
        P(None, None, "mp"),
        P(None, "mp"),
        P(None, None, "mp"),
        P(None, "mp"),
        P("mp", None),
        P(),
        P("mp", None),
        P(),
    )
    return jax.shard_map(
        functools.partial(per_device, mp=mesh.shape["mp"]),
        mesh=mesh,
        in_specs=placed,
        out_specs=(P("group", None), P("group", "mp"), P("group", "mp")),
        check_vma=False,
    )
```

time: 74 us -> 49.4 us (0.67)
  blocking collectives: 27.5 us -> 13.3 us
  Pallas kernels: 0 us -> 10.4 us
  local copies, waits for them, and re-layouts: 13.4 us -> 6.41 us
  other arithmetic: 7.76 us -> 1.55 us
  starting transfers between devices: 13.3 us -> 10.9 us
  between operations: 3.48 us -> 1.36 us
  waiting for transfers between devices: 6.54 us -> 4.86 us
  matrix products: 1.32 us -> 0 us
    all_gather x3 -> x0, blocking collectives: 16.1 us -> none  [the longest x1 5.42 us: advance(): lax.all_gather(hidden_part, 'mp', axis=1, tiled=True)]
    all_to_all x0 -> x1, blocking collectives: none -> 13.3 us  [per_device(): back = lax.all_to_all(values, everyone, 0, 0, tiled=True)]
    psum x1 -> x0, blocking collectives: 11.4 us -> none  [advance(): value_sum, advantage_sum = lax.psum((value_part, advantage_part), 'mp')]
    pallas_call x0 -> x4, Pallas kernels: none -> 10.4 us  [call(): pl.pallas_call(kernel, out_shape=out_shape, in_specs=specs, out_specs=jax...]
    all_to_all x2 -> x1, waiting for transfers between devices: 6.54 us -> 0.01 us  [per_device(): got = lax.all_to_all(send, everyone, 0, 0, tiled=True)]
    all_to_all x2 -> x1, starting transfers between devices: 13.3 us -> 7.33 us  [per_device(): got = lax.all_to_all(send, everyone, 0, 0, tiled=True)]
    ppermute x0 -> x4, waiting for transfers between devices: none -> 4.86 us  [gather_parts(): got = lax.ppermute(current, 'mp', pairs)]
    ppermute x0 -> x4, starting transfers between devices: none -> 3.62 us  [gather_parts(): got = lax.ppermute(current, 'mp', pairs)]
  transfers between devices with their start and end apart: 2 -> 5, of which waited for: 1 -> 2; matrix products, arithmetic and copies ran while one was open for 9% -> 12% of each run, Pallas kernels for 0% -> 0%
where the time goes in v1:
time: 49.4 us; the launch traced here: 48.8 us
  blocking collectives  13.3 us (27%)
  starting transfers between devices  10.9 us (22%)
  Pallas kernels  10.4 us (21%)
  local copies, waits for them, and re-layouts  6.41 us (13%)
  waiting for transfers between devices  4.86 us (10%)
  other arithmetic  1.55 us (3%)
  between operations  1.36 us (3%)
    all_to_all x1, blocking collectives, per_device(): back = lax.all_to_all(values, everyone, 0, 0, tiled=True)  13.3 us
    pallas_call x4, Pallas kernels, call(): pl.pallas_call(kernel, out_shape=out_shape, in_specs=specs, out_specs=jax...  10.4 us
    all_to_all x1, starting transfers between devices, per_device(): got = lax.all_to_all(send, everyone, 0, 0, tiled=True)  7.33 us
    unnamed x17, local copies, waits for them, and re-layouts  6.41 us
    ppermute x4, waiting for transfers between devices, gather_parts(): got = lax.ppermute(current, 'mp', pairs)  4.86 us
    ppermute x4, starting transfers between devices, gather_parts(): got = lax.ppermute(current, 'mp', pairs)  3.62 us
    concatenate x2, other arithmetic, gather_parts(): current = jnp.concatenate([current, got], axis=1)  1.55 us
  transfers between devices with their start and end apart: 5, of which 2 were waited for; matrix products, arithmetic and copies ran while one was open for 12% of the time, Pallas kernels for 0%

profile of v1, /device:TPU:0, one launch (start us, length us, event | category | flops | bytes accessed | tf_op | source)
XLA Modules:
  0.0 48.8 jit_solution(11790589872805849578)
XLA Ops:
  0.6 0.0 copy-start
  0.6 2.0 %shard_map.157 = (bf16[512,128]{1,0:T(8,128)(2,1)}, s32[64,128]{1,0:T(8,128)}, s32[2,128]{1,0:T(2,128)}) custom-call(s32[8]{0:T(128)} %counts_ref.1, s32[4,128]{1,0:T(4,128)} %bitcast.25, bf16[128,128]{1,0:T(8,128)(2,1)} %obs_ref.1), custom_call_target="tpu_custom_call" | custom-call | tf_op jit(solution)/shard_map/pallas_call | solution.py:180
  2.6 7.3 %all-to-all-start = ((bf16[32,16,128]{2,1,0:T(8,128)(2,1)}), bf16[32,16,128]{2,1,0:T(8,128)(2,1)S(1)}, u32[]{:S(2)}, u32[]{:S(2)}) async-start(bf16[32,16,128]{2,1,0:T(8,128)(2,1)} %bitcast.22), calls=%async_computation | async-start | bytes 262144 | tf_op jit(solution)/shard_map/all_to_all | solution.py:246
  10.0 1.8 %collective-permute-start = (bf16[64,256]{1,0:T(8,128)(2,1)}, bf16[64,256]{1,0:T(8,128)(2,1)S(1)}, u32[]{:S(2)}, u32[]{:S(2)}) collective-permute-start(bf16[64,256]{1,0:T(8,128)(2,1)} %refs_0_.1), channel_id=1, source_target_pairs={{0,2},{1,3},{2,0},{3,1},{4,6},{5,7},{6,4},{7,5},{8,10},{9,11},{10,... | collective-permute-start | bytes 98312 | tf_op jit(solution)/shard_map/ppermute | solution.py:197
  11.8 2.5 %collective-permute-done.refs_1_ = bf16[64,256]{1,0:T(8,128)(2,1)S(1)} collective-permute-done((bf16[64,256]{1,0:T(8,128)(2,1)}, bf16[64,256]{1,0:T(8,128)(2,1)S(1)}, u32[]{:S(2)}, u32[]{:S(2)}) %collective-permute-start) | collective-permute-done | bytes 32800 | tf_op jit(solution)/shard_map/ppermute | solution.py:197
  14.3 0.0 copy-start.3
  14.3 0.8 %pad_maximum_fusion = bf16[64,512]{1,0:T(8,128)(2,1)S(1)} fusion(bf16[64,256]{1,0:T(8,128)(2,1)S(1)} %collective-permute-done.refs_1_, bf16[64,256]{1,0:T(8,128)(2,1)} %refs_0_.1), kind=kLoop, calls=%fused_computation.1 | loop fusion | flops 131072 | bytes 131072 | tf_op jit(solution)/shard_map/concatenate | solution.py:203
  15.1 0.0 collective-permute-start.1
  15.1 2.4 %copy.17 = bf16[64,8,4,256]{3,1,2,0:T(8,128)(2,1)} copy(bf16[64,8,4,256]{3,2,1,0:T(4,128)(2,1)} %bitcast.19) | data formatting | bytes 2097152
  17.5 0.0 copy-done
  17.5 1.8 %copy.18 = bf16[128,8,4,256]{3,1,2,0:T(8,128)(2,1)} copy(bf16[128,8,4,256]{3,2,1,0:T(4,128)(2,1)S(1)} %bitcast.17) | data formatting | bytes 4194304
  19.4 0.0 copy-done.3
  19.4 0.0 copy-start.1
  19.4 0.0 collective-permute-done.1.refs_2_
  19.4 0.0 copy-start.5
  19.4 0.0 all-to-all-done
  19.4 0.0 copy-start.2
  19.4 0.6 %copy-done.5 = bf16[64,512]{1,0:T(8,128)(2,1)} copy-done((bf16[64,512]{1,0:T(8,128)(2,1)}, bf16[64,512]{1,0:T(8,128)(2,1)S(1)}, u32[]{:S(2)}) %copy-start.5) | copy-done | bytes 65560
  20.0 0.1 copy-done.2
  20.1 3.5 %shard_map.158 = (bf16[64,256]{1,0:T(8,128)(2,1)}, bf16[64,256]{1,0:T(8,128)(2,1)}) custom-call(s32[64,128]{1,0:T(8,128)} %get-tuple-element.9.base_ref, bf16[512,128]{1,0:T(8,128)(2,1)} %bitcast.21, bf16[64,256]{1,0:T(8,128)(2,1)} %refs_0_.1, bf16[64,256]{1,0:T(8,128)(2,1)} %copy-done.3, bf16[64,512]{1,0:T(8,128)(2,1)} %copy-done.5, ...), custom_call_target="tpu_custom_call" | custom-call | tf_op jit(solution)/shard_map/pallas_call | solution.py:180
  23.6 1.8 %collective-permute-start.2 = (bf16[64,256]{1,0:T(8,128)(2,1)}, bf16[64,256]{1,0:T(8,128)(2,1)S(1)}, u32[]{:S(2)}, u32[]{:S(2)}) collective-permute-start(bf16[64,256]{1,0:T(8,128)(2,1)} %get-tuple-element.6.refs_0_), channel_id=1, source_target_pairs={{0,2},{1,3},{2,0},{3,1},{4,6},{5,7},{6,4},{7,5},{8,10},{9,11},{10,... | collective-permute-start | bytes 98312 | tf_op jit(solution)/shard_map/ppermute | solution.py:197
  25.4 2.3 %collective-permute-done.2.refs_1_ = bf16[64,256]{1,0:T(8,128)(2,1)S(1)} collective-permute-done((bf16[64,256]{1,0:T(8,128)(2,1)}, bf16[64,256]{1,0:T(8,128)(2,1)S(1)}, u32[]{:S(2)}, u32[]{:S(2)}) %collective-permute-start.2) | collective-permute-done | bytes 32800 | tf_op jit(solution)/shard_map/ppermute | solution.py:197
  27.7 0.0 copy-start.4
  27.7 0.8 %pad_maximum_fusion.1 = bf16[64,512]{1,0:T(8,128)(2,1)S(1)} fusion(bf16[64,256]{1,0:T(8,128)(2,1)S(1)} %collective-permute-done.2.refs_1_, bf16[64,256]{1,0:T(8,128)(2,1)} %get-tuple-element.6.refs_0_), kind=kLoop, calls=%fused_computation.2 | loop fusion | flops 131072 | bytes 131072 | tf_op jit(solution)/shard_map/concatenate | solution.py:203
  28.5 0.0 collective-permute-start.3
  28.5 0.0 copy-done.1
  28.5 0.9 %copy.21 = bf16[128,8,2,128]{3,1,2,0:T(8,128)(2,1)} copy(bf16[128,8,2,128]{3,2,1,0:T(2,128)(2,1)S(1)} %bitcast.20) | data formatting | bytes 1048576
  30.0 0.0 collective-permute-done.3.refs_2_
  30.0 0.0 copy-start.6
  30.0 0.0 copy-done.4
  30.1 0.6 %copy-done.6 = bf16[64,512]{1,0:T(8,128)(2,1)} copy-done((bf16[64,512]{1,0:T(8,128)(2,1)}, bf16[64,512]{1,0:T(8,128)(2,1)S(1)}, u32[]{:S(2)}) %copy-start.6) | copy-done | bytes 65560
  30.6 2.7 %shard_map.159 = f32[32,1,384]{2,1,0:T(1,128)} custom-call(s32[64,128]{1,0:T(8,128)} %get-tuple-element.9.base_ref, bf16[64,256]{1,0:T(8,128)(2,1)} %get-tuple-element.6.refs_0_, bf16[64,256]{1,0:T(8,128)(2,1)} %copy-done.4, bf16[64,512]{1,0:T(8,128)(2,1)} %copy-done.6, bf16[1024,256]{1,0:T(8,128)(2,1)} %bitcast.18, f32[2,128]{1,0:T(2,128)} %refs_4_.1, ...), custom_call_target="tpu_custom_call" | custom-call | tf_op jit(solution)/shard_map/pallas_call | solution.py:180
  33.3 13.3 %all_to_all.16.rows_ref = f32[32,1,384]{2,1,0:T(1,128)} all-to-all(f32[32,1,384]{2,1,0:T(1,128)} %shard_map.159), channel_id=1, replica_groups=mesh['group'=8,'mp'=4] {'group','mp'}, dimensions={0} | all-to-all | bytes 98304 | tf_op jit(solution)/shard_map/all_to_all | solution.py:290
  46.7 2.2 %shard_map.160 = f32[18,128]{1,0:T(8,128)} custom-call(s32[2,128]{1,0:T(2,128)} %get-tuple-element.8.slot_ref, f32[32,1,384]{2,1,0:T(1,128)} %all_to_all.16.rows_ref), custom_call_target="tpu_custom_call" | custom-call | tf_op jit(solution)/shard_map/pallas_call | solution.py:180
Async XLA Ops:
  0.6 16.9 %copy-start = (bf16[1024,4,256]{2,1,0:T(4,128)(2,1)S(1)}, bf16[1024,4,256]{2,1,0:T(4,128)(2,1)}, u32[]{:S(2)}) copy-start(bf16[1024,4,256]{2,1,0:T(4,128)(2,1)} %param.20) | copy-start | bytes 6291460
  2.6 16.7 %all-to-all-start = ((bf16[32,16,128]{2,1,0:T(8,128)(2,1)}), bf16[32,16,128]{2,1,0:T(8,128)(2,1)S(1)}, u32[]{:S(2)}, u32[]{:S(2)}) async-start(bf16[32,16,128]{2,1,0:T(8,128)(2,1)} %bitcast.22), calls=%async_computation | async-start | bytes 262144 | tf_op jit(solution)/shard_map/all_to_all | solution.py:246
  10.0 4.3 %collective-permute-start = (bf16[64,256]{1,0:T(8,128)(2,1)}, bf16[64,256]{1,0:T(8,128)(2,1)S(1)}, u32[]{:S(2)}, u32[]{:S(2)}) collective-permute-start(bf16[64,256]{1,0:T(8,128)(2,1)} %refs_0_.1), channel_id=1, source_target_pairs={{0,2},{1,3},{2,0},{3,1},{4,6},{5,7},{6,4},{7,5},{8,10},{9,11},{10,... | collective-permute-start | bytes 98312 | tf_op jit(solution)/shard_map/ppermute | solution.py:197
  14.3 5.0 %copy-start.3 = (bf16[64,256]{1,0:T(8,128)(2,1)}, bf16[64,256]{1,0:T(8,128)(2,1)S(1)}, u32[]{:S(2)}) copy-start(bf16[64,256]{1,0:T(8,128)(2,1)S(1)} %collective-permute-done.refs_1_) | copy-start | bytes 98308
  15.1 4.3 %collective-permute-start.1 = (bf16[64,512]{1,0:T(8,128)(2,1)S(1)}, bf16[64,512]{1,0:T(8,128)(2,1)S(1)}, u32[]{:S(2)}, u32[]{:S(2)}) collective-permute-start(bf16[64,512]{1,0:T(8,128)(2,1)S(1)} %pad_maximum_fusion), channel_id=1, source_target_pairs={{0,1},{1,0},{2,3},{3,2},{4,5},{5,4},{6,7},{7,6},{8,9},{9,8},{10,11... | collective-permute-start | bytes 196616 | tf_op jit(solution)/shard_map/ppermute | solution.py:197
  19.4 9.1 %copy-start.1 = (bf16[1024,2,128]{2,1,0:T(2,128)(2,1)S(1)}, bf16[1024,2,128]{2,1,0:T(2,128)(2,1)}, u32[]{:S(2)}) copy-start(bf16[1024,2,128]{2,1,0:T(2,128)(2,1)} %param.22) | copy-start | bytes 1572868
  19.4 0.6 %copy-start.5 = (bf16[64,512]{1,0:T(8,128)(2,1)}, bf16[64,512]{1,0:T(8,128)(2,1)S(1)}, u32[]{:S(2)}) copy-start(bf16[64,512]{1,0:T(8,128)(2,1)S(1)} %collective-permute-done.1.refs_2_) | copy-start | bytes 196612
  19.4 0.7 %copy-start.2 = (bf16[32,16,128]{2,1,0:T(8,128)(2,1)}, bf16[32,16,128]{2,1,0:T(8,128)(2,1)S(1)}, u32[]{:S(2)}) copy-start(bf16[32,16,128]{2,1,0:T(8,128)(2,1)S(1)} %all-to-all-done) | copy-start | bytes 393220
  23.6 4.1 %collective-permute-start.2 = (bf16[64,256]{1,0:T(8,128)(2,1)}, bf16[64,256]{1,0:T(8,128)(2,1)S(1)}, u32[]{:S(2)}, u32[]{:S(2)}) collective-permute-start(bf16[64,256]{1,0:T(8,128)(2,1)} %get-tuple-element.6.refs_0_), channel_id=1, source_target_pairs={{0,2},{1,3},{2,0},{3,1},{4,6},{5,7},{6,4},{7,5},{8,10},{9,11},{10,... | collective-permute-start | bytes 98312 | tf_op jit(solution)/shard_map/ppermute | solution.py:197
  27.7 2.3 %copy-start.4 = (bf16[64,256]{1,0:T(8,128)(2,1)}, bf16[64,256]{1,0:T(8,128)(2,1)S(1)}, u32[]{:S(2)}) copy-start(bf16[64,256]{1,0:T(8,128)(2,1)S(1)} %collective-permute-done.2.refs_1_) | copy-start | bytes 98308
  28.5 1.5 %collective-permute-start.3 = (bf16[64,512]{1,0:T(8,128)(2,1)S(1)}, bf16[64,512]{1,0:T(8,128)(2,1)S(1)}, u32[]{:S(2)}, u32[]{:S(2)}) collective-permute-start(bf16[64,512]{1,0:T(8,128)(2,1)S(1)} %pad_maximum_fusion.1), channel_id=1, source_target_pairs={{0,1},{1,0},{2,3},{3,2},{4,5},{5,4},{6,7},{7,6},{8,9},{9,8},{10,11... | collective-permute-start | bytes 196616 | tf_op jit(solution)/shard_map/ppermute | solution.py:197
  30.0 0.6 %copy-start.6 = (bf16[64,512]{1,0:T(8,128)(2,1)}, bf16[64,512]{1,0:T(8,128)(2,1)S(1)}, u32[]{:S(2)}) copy-start(bf16[64,512]{1,0:T(8,128)(2,1)S(1)} %collective-permute-done.3.refs_2_) | copy-start | bytes 196612

commit v2 on v1

--- a/solution.py
+++ b/solution.py
@@ -1,4 +1,5 @@
 import functools
+import math
 
 import jax
 import jax.numpy as jnp
@@ -7,12 +8,12 @@
 from jax.experimental.pallas import tpu as pltpu
 from jax.sharding import PartitionSpec as P
 
+
 BF16 = jnp.bfloat16
 F32 = jnp.float32
 I32 = jnp.int32
-EXACT = lax.Precision.HIGHEST
 VMEM = pl.BlockSpec(memory_space=pltpu.VMEM)
-SMEM = pl.BlockSpec(memory_space=pltpu.SMEM)
+HBM = pl.BlockSpec(memory_space=pltpu.HBM)
 
 
 def iota(shape, axis):
@@ -31,13 +32,24 @@
     return jnp.where(mask, 1.0, 0.0).astype(BF16)
 
 
-def dot(left, right, contract=((1,), (0,)), precision=None):
-    return lax.dot_general(
-        left, right, (contract, ((), ())), precision=precision, preferred_element_type=F32
-    )
-
-
-def route_kernel(mp, per_owner, counts_ref, order_ref, obs_ref, send_ref, base_ref, slot_ref):
+def dot(left, right, contract=((1,), (0,))):
+    return lax.dot_general(left, right, (contract, ((), ())), preferred_element_type=F32)
+
+
+def route_kernel(
+    mp, per_owner, counts_from, order_from, obs_from, send_ref, base_ref, slot_ref,
+    counts_ref, order_ref, obs_ref, sems,
+):
+    copies = [
+        pltpu.make_async_copy(source, held, sems.at[index])
+        for index, (source, held) in enumerate(
+            ((counts_from, counts_ref), (order_from, order_ref), (obs_from, obs_ref))
+        )
+    ]
+    for copy in copies:
+        copy.start()
+    copies[0].wait()
+    copies[1].wait()
     blocks, capacity = order_ref.shape
     batches = counts_ref.shape[0]
     per_pair = capacity // batches
@@ -68,6 +80,7 @@
     row_ids, rank_ids = split(iota((mp * capacity, capacity), 0), per_pair)
     row_owner, _ = split(row_ids, mp)
     target = jnp.where(filled, owner * per_pair + rank, -1)
+    copies[2].wait()
     send_ref[...] = dot(
         one_hot(row_owner * per_pair + rank_ids == target), obs_ref[...]
     ).astype(send_ref.dtype)
@@ -112,9 +125,9 @@
             input_ref[part * features : (part + 1) * features, :],
         )
         gates = term if gates is None else gates + term
-    for (ref, column), offset in zip(hidden_refs, offsets):
+    for ref, offset in zip(hidden_refs, offsets):
         rows = pl.ds(pl.multiple_of(jnp.bitwise_xor(me, offset) * units, units), units)
-        gates = gates + dot(ref[:, column : column + units], state_ref[rows, :])
+        gates = gates + dot(ref[...], state_ref[rows, :])
     gate = [
         gates[:, k * units : (k + 1) * units] + bias_ref[k : k + 1, :] for k in range(4)
     ]
@@ -123,88 +136,106 @@
     hidden_ref[...] = (jax.nn.sigmoid(gate[3]) * jnp.tanh(cell)).astype(BF16)
 
 
+def pieces(values):
+    high = values.astype(BF16)
+    rest = values - high.astype(F32)
+    middle = rest.astype(BF16)
+    low = (rest - middle.astype(F32)).astype(BF16)
+    return jnp.concatenate([high, middle, low], axis=0)
+
+
+def stride_of(actions):
+    return -(-actions // 8) * 8
+
+
 def head_kernel(
-    mp, per_pair, offsets, base_ref, hidden_refs, head_ref, head_bias_ref, value_ref, value_bias_ref,
-    advantage_ref, advantage_bias_ref, send_ref,
+    mp, per_pair, actions, offsets, base_ref, hidden_refs, cell_ref, head_ref,
+    bias_ref, value_ref, advantage_ref, send_ref, hidden_to, cell_to, sems,
 ):
+    copies = [
+        pltpu.make_async_copy(hidden_refs[0], hidden_to, sems.at[0]),
+        pltpu.make_async_copy(cell_ref, cell_to, sems.at[1]),
+    ]
+    for copy in copies:
+        copy.start()
     per_owner = base_ref.shape[0]
     units = head_ref.shape[0] // mp
-    width = head_bias_ref.shape[1]
-    actions = advantage_ref.shape[0]
     me = lax.axis_index("mp")
     total = None
-    for (ref, column), offset in zip(hidden_refs, offsets):
+    for ref, offset in zip(hidden_refs, offsets):
         rows = pl.ds(pl.multiple_of(jnp.bitwise_xor(me, offset) * units, units), units)
-        term = dot(ref[:, column : column + units], head_ref[rows, :])
+        term = dot(ref[...], head_ref[rows, :])
         total = term if total is None else total + term
-    value_stream = jnp.maximum(total[:, :width] + head_bias_ref[0:1, :], 0.0).astype(BF16)
-    advantage_stream = jnp.maximum(total[:, width:] + head_bias_ref[1:2, :], 0.0).astype(BF16)
-    value = jnp.sum(
-        value_stream.astype(F32) * value_ref[...].astype(F32), axis=1, keepdims=True
-    )
-    advantage = dot(advantage_stream, advantage_ref[...], ((1,), (1,)))
+    both = total.shape[1]
+    width = both // 2
+    lanes = send_ref.shape[2]
+    streams = jnp.maximum(total + bias_ref[:, :both], 0.0).astype(BF16)
     first = jnp.where(me == 0, 1.0, 0.0)
-    advantage = advantage + advantage_bias_ref[...] * first
-    value = value + value_bias_ref[0] * first
+    advantage = dot(streams[:, width:], advantage_ref[...], ((1,), (1,)))
+    advantage = advantage + bias_ref[:, both : both + actions] * first
+    value = streams[:, :width].astype(F32) * value_ref[...].astype(F32)
+    value = jnp.sum(value, axis=1, keepdims=True) + bias_ref[:, both + 128 : both + 129] * first
     mixed = value + advantage - jnp.sum(advantage, axis=1, keepdims=True) * (1.0 / actions)
-    lanes = send_ref.shape[2]
-    lane_rank, lane_action = split(iota((actions, lanes), 1), actions)
-    spread = dot(
-        mixed,
-        jnp.where(
-            (lane_action == iota((actions, lanes), 0)) & (lane_rank < per_pair), 1.0, 0.0
-        ),
-        precision=EXACT,
-    )
+    lane_rank, lane_action = split(iota((actions, lanes), 1), stride_of(actions))
+    to_lane = one_hot((lane_action == iota((actions, lanes), 0)) & (lane_rank < per_pair))
+    spread = dot(pieces(mixed), to_lane)
+    spread = spread[:per_owner] + spread[per_owner : 2 * per_owner] + spread[2 * per_owner :]
     batch, rank = split(base_ref[:, 0:1], mp * per_pair)
-    spread = jnp.where(split(iota((per_owner, lanes), 1), actions)[0] == rank, spread, 0.0)
+    lane_rank, _ = split(iota((1, lanes), 1), stride_of(actions))
+    spread = jnp.where(lane_rank == rank, spread, 0.0)
     rows = send_ref.shape[0]
-    to_row = jnp.where(split(iota((per_owner, rows), 1), mp)[0] == batch, 1.0, 0.0)
-    send_ref[:, 0, :] = dot(to_row, spread, ((0,), (0,)), precision=EXACT)
+    to_row = one_hot(split(iota((per_owner, rows), 1), mp)[0] == batch)
+    to_row = jnp.concatenate([to_row] * 3, axis=0)
+    send_ref[:, 0, :] = dot(to_row, pieces(spread), ((0,), (0,)))
+    for copy in copies:
+        copy.wait()
 
 
 def place_kernel(mp, per_pair, slot_ref, rows_ref, out_ref):
     actions, capacity = out_ref.shape
-    rows, _, lanes = rows_ref.shape
+    rows, _, _ = rows_ref.shape
+    stride = stride_of(actions)
     owner = slot_ref[0:1, :]
     rank = slot_ref[1:2, :]
-    to_slot = jnp.where(split(iota((rows, capacity), 0), mp)[0] == owner, 1.0, 0.0)
-    spread = dot(rows_ref[:, 0, :], to_slot, ((0,), (0,)), precision=EXACT)
-    spread = jnp.where(split(iota((lanes, capacity), 0), actions)[0] == rank, spread, 0.0)
-    lane_rank, lane_action = split(iota((actions, lanes), 1), actions)
-    pick = jnp.where((lane_action == iota((actions, lanes), 0)) & (lane_rank < per_pair), 1.0, 0.0)
-    out_ref[...] = dot(pick, spread, precision=EXACT)
-
-
-def call(kernel, out_shape, specs, *args):
+    to_slot = one_hot(split(iota((rows, capacity), 0), mp)[0] == owner)
+    to_slot = jnp.concatenate([to_slot] * 3, axis=0)
+    spread = dot(pieces(rows_ref[:, 0, :]), to_slot, ((0,), (0,)))
+    total = jnp.zeros((stride, capacity), F32)
+    for index in range(per_pair):
+        total = total + jnp.where(rank == index, spread[index * stride : (index + 1) * stride, :], 0.0)
+    out_ref[...] = total[:actions, :]
+
+
+def call(kernel, out_shape, specs, *args, out_specs=None, scratch=(), whole=False):
+    held = [math.prod(x.shape) * x.dtype.itemsize for x in (*args, *jax.tree.leaves(out_shape))]
     return pl.pallas_call(
         kernel,
         out_shape=out_shape,
         in_specs=specs,
-        out_specs=jax.tree.map(lambda _: VMEM, out_shape),
+        out_specs=out_specs or jax.tree.map(lambda _: VMEM, out_shape),
+        scratch_shapes=list(scratch),
+        compiler_params=pltpu.CompilerParams(
+            vmem_limit_bytes=None if whole else 2 * sum(held) + (4 << 20)
+        ),
     )(*args)
 
 
 def gather_parts(part, mp):
     arrays = [part]
-    places = [(0, 0)]
     offsets = [0]
-    width = part.shape[1]
-    current = part
     distance = mp // 2
     while distance:
         pairs = [(device, device ^ distance) for device in range(mp)]
-        got = lax.ppermute(current, "mp", pairs)
-        places += [(len(arrays), k * width) for k in range(got.shape[1] // width)]
-        arrays.append(got)
+        got = []
+        for array in arrays:
+            got.append(lax.ppermute(array, "mp", pairs))
+        arrays += got
         offsets += [offset ^ distance for offset in offsets]
         distance //= 2
-        if distance:
-            current = jnp.concatenate([current, got], axis=1)
-    return arrays, places, offsets
-
-
-def per_device(
+    return arrays, offsets
+
+
+def step(
     observations,
     hidden_state,
     cell_state,
@@ -230,7 +261,11 @@
     rows = batches * mp
     everyone = ("group", "mp")
 
-    hidden_arrays, hidden_places, offsets = gather_parts(hidden_state, mp)
+    stride = stride_of(actions)
+    lanes = -(-per_pair * stride // 128) * 128
+    order = arrival_order.reshape(-1, capacity)
+
+    hidden_arrays, offsets = gather_parts(hidden_state, mp)
     send, base, slot = call(
         functools.partial(route_kernel, mp, per_owner),
         (
@@ -238,25 +273,29 @@
             jax.ShapeDtypeStruct((per_owner, 128), I32),
             jax.ShapeDtypeStruct((2, capacity), I32),
         ),
-        [SMEM, VMEM, VMEM],
+        [HBM, HBM, HBM],
         batch_counts,
-        arrival_order.reshape(-1, capacity),
+        order,
         observations,
+        scratch=(
+            pltpu.SMEM(batch_counts.shape, I32),
+            pltpu.VMEM(order.shape, I32),
+            pltpu.VMEM(observations.shape, BF16),
+            pltpu.SemaphoreType.DMA((3,)),
+        ),
+        whole=True,
     )
     got = lax.all_to_all(send, everyone, 0, 0, tiled=True)
 
     count = len(hidden_arrays)
 
     def cell_body(base_ref, rows_ref, *refs):
-        places = [(refs[array], column) for array, column in hidden_places]
-        cell_kernel(mp, per_pair, offsets, base_ref, rows_ref, places, *refs[count:])
-
-    new_hidden, new_cell = call(
+        cell_kernel(mp, per_pair, offsets, base_ref, rows_ref, refs[:count], *refs[count:])
+
+    state = jax.ShapeDtypeStruct((per_owner, units), BF16)
+    next_hidden, next_cell = call(
         cell_body,
-        (
-            jax.ShapeDtypeStruct((per_owner, units), BF16),
-            jax.ShapeDtypeStruct((per_owner, units), BF16),
-        ),
+        (state, state),
         [VMEM] * (6 + count),
         base,
         got,
@@ -267,25 +306,27 @@
         gate_bias,
     )
 
-    next_arrays, next_places, _ = gather_parts(new_hidden, mp)
+    next_arrays, _ = gather_parts(next_hidden, mp)
 
     def head_body(base_ref, *refs):
-        places = [(refs[array], column) for array, column in next_places]
-        head_kernel(mp, per_pair, offsets, base_ref, places, *refs[count:])
-
-    lanes = -(-per_pair * actions // 128) * 128
-    values = call(
+        head_kernel(mp, per_pair, actions, offsets, base_ref, refs[:count], *refs[count:])
+
+    bias = jnp.concatenate(
+        [head_bias.reshape(-1), jnp.pad(advantage_bias, (0, -actions % 128)), value_bias]
+    )
+    values, new_hidden, new_cell = call(
         head_body,
-        jax.ShapeDtypeStruct((rows, 1, lanes), F32),
-        [VMEM] * (4 + count) + [SMEM, VMEM, VMEM],
+        (jax.ShapeDtypeStruct((rows, 1, lanes), F32), state, state),
+        [VMEM] * (6 + count),
         base,
         *next_arrays,
+        next_cell,
         head_weight.reshape(head_weight.shape[0], -1),
-        head_bias,
+        bias.reshape(1, -1),
         value_weight.T,
-        value_bias,
         advantage_weight.T,
-        advantage_bias.reshape(1, -1),
+        out_specs=(VMEM, HBM, HBM),
+        scratch=(pltpu.SemaphoreType.DMA((2,)),),
     )
     back = lax.all_to_all(values, everyone, 0, 0, tiled=True)
     placed = call(
@@ -316,7 +357,7 @@
         P(),
     )
     return jax.shard_map(
-        functools.partial(per_device, mp=mesh.shape["mp"]),
+        functools.partial(step, mp=mesh.shape["mp"]),
         mesh=mesh,
         in_specs=placed,
         out_specs=(P("group", None), P("group", "mp"), P("group", "mp")),

time: 49.4 us -> 37.7 us (0.76)
  Pallas kernels: 10.4 us -> 4.65 us
  local copies, waits for them, and re-layouts: 6.41 us -> 2.08 us
  waiting for transfers between devices: 4.86 us -> 8.2 us
  blocking collectives: 13.3 us -> 11.3 us
  other arithmetic: 1.55 us -> 0.01 us
  starting transfers between devices: 10.9 us -> 9.67 us
    pallas_call x4, Pallas kernels: 10.4 us -> 4.65 us  [call(): pl.pallas_call(kernel, out_shape=out_shape, in_specs=specs, out_specs=out...]
    unnamed x17 -> x25, local copies, waits for them, and re-layouts: 6.41 us -> 2.08 us
    all_to_all x1, blocking collectives: 13.3 us -> 11.3 us  [step(): back = lax.all_to_all(values, everyone, 0, 0, tiled=True)]
    all_to_all x1, waiting for transfers between devices: 0.01 us -> 1.8 us  [step(): got = lax.all_to_all(send, everyone, 0, 0, tiled=True)]
    concatenate x2 -> x1, other arithmetic: 1.55 us -> 0.01 us  [step(): jnp.concatenate([head_bias.reshape(-1), jnp.pad(advantage_bias, (0, -acti...]
    ppermute x4 -> x6, waiting for transfers between devices: 4.86 us -> 6.4 us  [gather_parts(): got.append(lax.ppermute(array, 'mp', pairs))]
    ppermute x4 -> x6, starting transfers between devices: 3.62 us -> 2.34 us  [gather_parts(): got.append(lax.ppermute(array, 'mp', pairs))]
  transfers between devices with their start and end apart: 5 -> 7, of which waited for: 2 -> 4; matrix products, arithmetic and copies ran while one was open for 12% -> 5% of each run, Pallas kernels for 0% -> 0%
where the time goes in v2:
time: 37.7 us; the launch traced here: 37.4 us
  blocking collectives  11.3 us (30%)
  starting transfers between devices  9.67 us (26%)
  waiting for transfers between devices  8.2 us (22%)
  Pallas kernels  4.65 us (12%)
  local copies, waits for them, and re-layouts  2.08 us (6%)
  between operations  1.48 us (4%)
    all_to_all x1, blocking collectives, step(): back = lax.all_to_all(values, everyone, 0, 0, tiled=True)  11.3 us
    all_to_all x1, starting transfers between devices, step(): got = lax.all_to_all(send, everyone, 0, 0, tiled=True)  7.33 us
    ppermute x6, waiting for transfers between devices, gather_parts(): got.append(lax.ppermute(array, 'mp', pairs))  6.4 us
    pallas_call x4, Pallas kernels, call(): pl.pallas_call(kernel, out_shape=out_shape, in_specs=specs, out_specs=out...  4.65 us
    ppermute x6, starting transfers between devices, gather_parts(): got.append(lax.ppermute(array, 'mp', pairs))  2.34 us
    unnamed x25, local copies, waits for them, and re-layouts  2.08 us
    all_to_all x1, waiting for transfers between devices, step(): got = lax.all_to_all(send, everyone, 0, 0, tiled=True)  1.8 us
  transfers between devices with their start and end apart: 7, of which 4 were waited for; matrix products, arithmetic and copies ran while one was open for 5% of the time, Pallas kernels for 0%

profile of v2, /device:TPU:0, one launch (start us, length us, event | category | flops | bytes accessed | tf_op | source)
XLA Modules:
  0.0 37.4 jit_solution(7614315050753752711)
XLA Ops:
  0.6 1.8 %shard_map.157 = (bf16[512,128]{1,0:T(8,128)(2,1)}, s32[64,128]{1,0:T(8,128)}, s32[2,128]{1,0:T(2,128)}) custom-call(s32[8]{0:T(128)} %counts_from.1, s32[4,128]{1,0:T(4,128)} %bitcast.28, bf16[128,128]{1,0:T(8,128)(2,1)} %obs_from.1), custom_call_target="tpu_custom_call" | custom-call | tf_op jit(solution)/shard_map/pallas_call | solution.py:211
  2.5 7.3 %all-to-all-start = ((bf16[32,16,128]{2,1,0:T(8,128)(2,1)}), bf16[32,16,128]{2,1,0:T(8,128)(2,1)S(1)}, u32[]{:S(2)}, u32[]{:S(2)}) async-start(bf16[32,16,128]{2,1,0:T(8,128)(2,1)} %bitcast.26), calls=%async_computation | async-start | bytes 262144 | tf_op jit(solution)/shard_map/all_to_all | solution.py:288
  9.8 0.0 copy-start.7
  9.8 1.8 %collective-permute-start = (bf16[64,256]{1,0:T(8,128)(2,1)}, bf16[64,256]{1,0:T(8,128)(2,1)S(1)}, u32[]{:S(2)}, u32[]{:S(2)}) collective-permute-start(bf16[64,256]{1,0:T(8,128)(2,1)} %refs_0_.1), channel_id=1, source_target_pairs={{0,2},{1,3},{2,0},{3,1},{4,6},{5,7},{6,4},{7,5},{8,10},{9,11},{10,... | collective-permute-start | bytes 98312 | tf_op jit(solution)/shard_map/ppermute | solution.py:231
  11.7 0.0 collective-permute-start.1
  11.7 2.5 %collective-permute-done.refs_1_ = bf16[64,256]{1,0:T(8,128)(2,1)S(1)} collective-permute-done((bf16[64,256]{1,0:T(8,128)(2,1)}, bf16[64,256]{1,0:T(8,128)(2,1)S(1)}, u32[]{:S(2)}, u32[]{:S(2)}) %collective-permute-start) | collective-permute-done | bytes 32800 | tf_op jit(solution)/shard_map/ppermute | solution.py:231
  14.2 0.0 collective-permute-start.2
  14.2 1.4 %copy.17 = bf16[64,8,4,256]{3,1,2,0:T(8,128)(2,1)S(1)} copy(bf16[64,8,4,256]{3,2,1,0:T(4,128)(2,1)} %bitcast.24) | data formatting | bytes 2097152
  15.6 0.0 copy-done.7
  15.6 0.0 copy-start
  15.6 0.0 copy-start.1
  15.6 0.0 copy-start.2
  15.7 0.0 copy-start.4
  15.7 0.5 %copy.18 = bf16[128,8,4,256]{3,1,2,0:T(8,128)(2,1)S(1)} copy(bf16[128,8,4,256]{3,2,1,0:T(4,128)(2,1)S(1)} %bitcast.23) | data formatting | bytes 4194304
  16.2 0.0 copy-start.9
  16.2 0.0 copy-start.10
  16.2 0.0 collective-permute-done.1.refs_2_
  16.2 0.0 collective-permute-done.2.refs_3_
  16.2 1.8 %all-to-all-done = bf16[32,16,128]{2,1,0:T(8,128)(2,1)S(1)} async-done(((bf16[32,16,128]{2,1,0:T(8,128)(2,1)}), bf16[32,16,128]{2,1,0:T(8,128)(2,1)S(1)}, u32[]{:S(2)}, u32[]{:S(2)}) %all-to-all-start) | async-done | bytes 131104 | tf_op jit(solution)/shard_map/all_to_all | solution.py:288
  18.0 0.0 copy-start.8
  18.0 0.0 copy-done
  18.0 0.0 copy-done.1
  18.0 0.0 copy-done.2
  18.0 0.0 copy-done.4
  18.0 0.0 copy-start.3
  18.1 0.0 copy-start.6
  18.1 0.0 copy-start.5
  18.1 0.9 %shard_map.158 = (bf16[64,256]{1,0:T(8,128)(2,1)S(1)}, bf16[64,256]{1,0:T(8,128)(2,1)S(1)}) custom-call(s32[64,128]{1,0:T(8,128)S(1)} %copy-done, bf16[512,128]{1,0:T(8,128)(2,1)S(1)} %bitcast.19, bf16[64,256]{1,0:T(8,128)(2,1)S(1)} %copy-done.1, bf16[64,256]{1,0:T(8,128)(2,1)S(1)} %collective-permute-done.refs_1_, ...), custom_call_target="tpu_custom_call" | custom-call | tf_op jit(solution)/shard_map/pallas_call | solution.py:211
  19.0 0.4 %collective-permute-start.3 = (bf16[64,256]{1,0:T(8,128)(2,1)S(1)}, bf16[64,256]{1,0:T(8,128)(2,1)S(1)}, u32[]{:S(2)}, u32[]{:S(2)}) collective-permute-start(bf16[64,256]{1,0:T(8,128)(2,1)S(1)} %get-tuple-element.14.refs_0_), channel_id=1, source_target_pairs={{0,2},{1,3},{2,0},{3,1},{4,6},{5,7},{6,4},{7,5},{8,10},{9,11},{10,... | collective-permute-start | bytes 98312 | tf_op jit(solution)/shard_map/ppermute | solution.py:231
  20.0 0.1 collective-permute-start.4
  20.1 2.8 %collective-permute-done.3.refs_1_ = bf16[64,256]{1,0:T(8,128)(2,1)S(1)} collective-permute-done((bf16[64,256]{1,0:T(8,128)(2,1)S(1)}, bf16[64,256]{1,0:T(8,128)(2,1)S(1)}, u32[]{:S(2)}, u32[]{:S(2)}) %collective-permute-start.3) | collective-permute-done | bytes 32800 | tf_op jit(solution)/shard_map/ppermute | solution.py:231
  22.9 0.0 collective-permute-start.5
  22.9 0.0 copy-done.9
  22.9 0.0 copy-done.10
  23.0 0.0 copy-done.8
  23.0 0.1 copy.21
  23.1 0.0 collective-permute-done.4.refs_2_
  23.1 1.1 %collective-permute-done.5.refs_3_ = bf16[64,256]{1,0:T(8,128)(2,1)S(1)} collective-permute-done((bf16[64,256]{1,0:T(8,128)(2,1)S(1)}, bf16[64,256]{1,0:T(8,128)(2,1)S(1)}, u32[]{:S(2)}, u32[]{:S(2)}) %collective-permute-start.5) | collective-permute-done | bytes 32800 | tf_op jit(solution)/shard_map/ppermute | solution.py:231
  24.1 0.0 copy-done.3
  24.2 0.0 copy-done.6
  24.2 0.9 %shard_map.159 = (f32[32,1,384]{2,1,0:T(1,128)S(1)}, bf16[64,256]{1,0:T(8,128)(2,1)}, bf16[64,256]{1,0:T(8,128)(2,1)}) custom-call(s32[64,128]{1,0:T(8,128)S(1)} %copy-done, bf16[64,256]{1,0:T(8,128)(2,1)S(1)} %get-tuple-element.14.refs_0_, bf16[64,256]{1,0:T(8,128)(2,1)S(1)} %collective-permute-done.3.refs_1_, ...), custom_call_target="tpu_custom_call" | custom-call | tf_op jit(solution)/shard_map/pallas_call | solution.py:211
  25.1 11.3 %all_to_all.16.rows_ref = f32[32,1,384]{2,1,0:T(1,128)S(1)} all-to-all(f32[32,1,384]{2,1,0:T(1,128)S(1)} %get-tuple-element.16), channel_id=1, replica_groups=mesh['group'=8,'mp'=4] {'group','mp'}, dimensions={0} | all-to-all | bytes 98304 | tf_op jit(solution)/shard_map/all_to_all | solution.py:331
  36.4 0.0 copy-done.5
  36.4 1.0 %shard_map.160 = f32[18,128]{1,0:T(8,128)} custom-call(s32[2,128]{1,0:T(2,128)S(1)} %copy-done.5, f32[32,1,384]{2,1,0:T(1,128)S(1)} %all_to_all.16.rows_ref), custom_call_target="tpu_custom_call" | custom-call | tf_op jit(solution)/shard_map/pallas_call | solution.py:211
  (1 shorter events, 0.0 us)
Async XLA Ops:
  2.5 15.5 %all-to-all-start = ((bf16[32,16,128]{2,1,0:T(8,128)(2,1)}), bf16[32,16,128]{2,1,0:T(8,128)(2,1)S(1)}, u32[]{:S(2)}, u32[]{:S(2)}) async-start(bf16[32,16,128]{2,1,0:T(8,128)(2,1)} %bitcast.26), calls=%async_computation | async-start | bytes 262144 | tf_op jit(solution)/shard_map/all_to_all | solution.py:288
  9.8 5.8 %copy-start.7 = (bf16[1024,4,256]{2,1,0:T(4,128)(2,1)S(1)}, bf16[1024,4,256]{2,1,0:T(4,128)(2,1)}, u32[]{:S(2)}) copy-start(bf16[1024,4,256]{2,1,0:T(4,128)(2,1)} %param.20) | copy-start | bytes 6291460
  9.8 4.3 %collective-permute-start = (bf16[64,256]{1,0:T(8,128)(2,1)}, bf16[64,256]{1,0:T(8,128)(2,1)S(1)}, u32[]{:S(2)}, u32[]{:S(2)}) collective-permute-start(bf16[64,256]{1,0:T(8,128)(2,1)} %refs_0_.1), channel_id=1, source_target_pairs={{0,2},{1,3},{2,0},{3,1},{4,6},{5,7},{6,4},{7,5},{8,10},{9,11},{10,... | collective-permute-start | bytes 98312 | tf_op jit(solution)/shard_map/ppermute | solution.py:231
  11.7 4.5 %collective-permute-start.1 = (bf16[64,256]{1,0:T(8,128)(2,1)}, bf16[64,256]{1,0:T(8,128)(2,1)S(1)}, u32[]{:S(2)}, u32[]{:S(2)}) collective-permute-start(bf16[64,256]{1,0:T(8,128)(2,1)} %refs_0_.1), channel_id=1, source_target_pairs={{0,1},{1,0},{2,3},{3,2},{4,5},{5,4},{6,7},{7,6},{8,9},{9,8},{10,11... | collective-permute-start | bytes 98312 | tf_op jit(solution)/shard_map/ppermute | solution.py:231
  14.2 2.0 %collective-permute-start.2 = (bf16[64,256]{1,0:T(8,128)(2,1)S(1)}, bf16[64,256]{1,0:T(8,128)(2,1)S(1)}, u32[]{:S(2)}, u32[]{:S(2)}) collective-permute-start(bf16[64,256]{1,0:T(8,128)(2,1)S(1)} %collective-permute-done.refs_1_), channel_id=1, source_target_pairs={{0,1},{1,0},{2,3},{3,2},{4,5},{5,4},{6,7},{7,6},{8,9},{9,8},{10,11... | collective-permute-start | bytes 98312 | tf_op jit(solution)/shard_map/ppermute | solution.py:231
  15.6 2.4 %copy-start = (s32[64,128]{1,0:T(8,128)S(1)}, s32[64,128]{1,0:T(8,128)}, u32[]{:S(2)}) copy-start(s32[64,128]{1,0:T(8,128)} %get-tuple-element.12.base_ref) | copy-start | bytes 98308
  15.6 2.4 %copy-start.1 = (bf16[64,256]{1,0:T(8,128)(2,1)S(1)}, bf16[64,256]{1,0:T(8,128)(2,1)}, u32[]{:S(2)}) copy-start(bf16[64,256]{1,0:T(8,128)(2,1)} %refs_0_.1) | copy-start | bytes 98308
  15.6 2.4 %copy-start.2 = (bf16[64,256]{1,0:T(8,128)(2,1)S(1)}, bf16[64,256]{1,0:T(8,128)(2,1)}, u32[]{:S(2)}) copy-start(bf16[64,256]{1,0:T(8,128)(2,1)} %refs_4_.1) | copy-start | bytes 98308
  15.7 2.4 %copy-start.4 = (f32[4,256]{1,0:T(4,128)S(1)}, f32[4,256]{1,0:T(4,128)}, u32[]{:S(2)}) copy-start(f32[4,256]{1,0:T(4,128)} %refs_7_.1) | copy-start | bytes 12292
  16.2 6.8 %copy-start.9 = (f32[2,128]{1,0:T(2,128)S(1)}, f32[2,128]{1,0:T(2,128)}, u32[]{:S(2)}) copy-start(f32[2,128]{1,0:T(2,128)} %param.23) | copy-start | bytes 3076
  16.2 6.8 %copy-start.10 = (f32[18]{0:T(128)S(1)}, f32[18]{0:T(128)}, u32[]{:S(2)}) copy-start(f32[18]{0:T(128)} %param.27) | copy-start | bytes 220
  18.0 5.0 %copy-start.8 = (bf16[1024,2,128]{2,1,0:T(2,128)(2,1)S(1)}, bf16[1024,2,128]{2,1,0:T(2,128)(2,1)}, u32[]{:S(2)}) copy-start(bf16[1024,2,128]{2,1,0:T(2,128)(2,1)} %param.22) | copy-start | bytes 1572868
  18.0 6.1 %copy-start.3 = (bf16[128,18]{0,1:T(8,128)(2,1)S(1)}, bf16[128,18]{0,1:T(8,128)(2,1)}, u32[]{:S(2)}) copy-start(bf16[128,18]{0,1:T(8,128)(2,1)} %param.26) | copy-start | bytes 13828
  18.1 6.1 %copy-start.6 = (bf16[128,1]{0,1:T(2,128)(2,1)S(1)}, bf16[128,1]{0,1:T(2,128)(2,1)}, u32[]{:S(2)}) copy-start(bf16[128,1]{0,1:T(2,128)(2,1)} %param.24) | copy-start | bytes 772
  18.1 18.3 %copy-start.5 = (s32[2,128]{1,0:T(2,128)S(1)}, s32[2,128]{1,0:T(2,128)}, u32[]{:S(2)}) copy-start(s32[2,128]{1,0:T(2,128)} %get-tuple-element.11.slot_ref) | copy-start | bytes 3076
  19.0 4.0 %collective-permute-start.3 = (bf16[64,256]{1,0:T(8,128)(2,1)S(1)}, bf16[64,256]{1,0:T(8,128)(2,1)S(1)}, u32[]{:S(2)}, u32[]{:S(2)}) collective-permute-start(bf16[64,256]{1,0:T(8,128)(2,1)S(1)} %get-tuple-element.14.refs_0_), channel_id=1, source_target_pairs={{0,2},{1,3},{2,0},{3,1},{4,6},{5,7},{6,4},{7,5},{8,10},{9,11},{10,... | collective-permute-start | bytes 98312 | tf_op jit(solution)/shard_map/ppermute | solution.py:231
  20.0 3.1 %collective-permute-start.4 = (bf16[64,256]{1,0:T(8,128)(2,1)S(1)}, bf16[64,256]{1,0:T(8,128)(2,1)S(1)}, u32[]{:S(2)}, u32[]{:S(2)}) collective-permute-start(bf16[64,256]{1,0:T(8,128)(2,1)S(1)} %get-tuple-element.14.refs_0_), channel_id=1, source_target_pairs={{0,1},{1,0},{2,3},{3,2},{4,5},{5,4},{6,7},{7,6},{8,9},{9,8},{10,11... | collective-permute-start | bytes 98312 | tf_op jit(solution)/shard_map/ppermute | solution.py:231
  22.9 1.2 %collective-permute-start.5 = (bf16[64,256]{1,0:T(8,128)(2,1)S(1)}, bf16[64,256]{1,0:T(8,128)(2,1)S(1)}, u32[]{:S(2)}, u32[]{:S(2)}) collective-permute-start(bf16[64,256]{1,0:T(8,128)(2,1)S(1)} %collective-permute-done.3.refs_1_), channel_id=1, source_target_pairs={{0,1},{1,0},{2,3},{3,2},{4,5},{5,4},{6,7},{7,6},{8,9},{9,8},{10,11... | collective-permute-start | bytes 98312 | tf_op jit(solution)/shard_map/ppermute | solution.py:231

commit v3 on v2

v3 whole, which is shorter than its diff:
```python
import functools
import math

import jax
import jax.numpy as jnp
from jax import lax
from jax.experimental import pallas as pl
from jax.experimental.pallas import tpu as pltpu
from jax.sharding import PartitionSpec as P


BF16 = jnp.bfloat16
F32 = jnp.float32
I32 = jnp.int32
VMEM = pl.BlockSpec(memory_space=pltpu.VMEM)
SMEM = pl.BlockSpec(memory_space=pltpu.SMEM)
HBM = pl.BlockSpec(memory_space=pltpu.HBM)


def iota(shape, axis):
    return lax.broadcasted_iota(I32, shape, axis)


def split(values, divisor):
    if divisor & (divisor - 1) == 0:
        quotient = lax.shift_right_logical(values, jnp.int32(divisor.bit_length() - 1))
    else:
        quotient = ((values.astype(F32) + 0.5) * (1.0 / divisor)).astype(I32)
    return quotient, values - quotient * divisor


def one_hot(mask):
    return jnp.where(mask, 1.0, 0.0).astype(BF16)


def dot(left, right, contract=((1,), (0,))):
    return lax.dot_general(left, right, (contract, ((), ())), preferred_element_type=F32)


def pieces(values):
    high = values.astype(BF16)
    rest = values - high.astype(F32)
    middle = rest.astype(BF16)
    low = (rest - middle.astype(F32)).astype(BF16)
    return jnp.concatenate([high, middle, low], axis=0)


def stride_of(actions):
    return -(-actions // 8) * 8


def span_ends(counts_ref):
    ends = []
    total = jnp.int32(0)
    for batch in range(counts_ref.shape[0]):
        total = total + counts_ref[batch]
        ends.append(total)
    return ends


def before(size):
    return one_hot(iota((size, size), 0) < iota((size, size), 1))


def route_kernel(
    mp, per_owner, counts_from, order_from, obs_from, input_from, send_to, slot_ref,
    input_ref, counts_ref, order_ref, obs_ref, send_ref, sems,
):
    copies = [
        pltpu.make_async_copy(source, held, sems.at[index])
        for index, (source, held) in enumerate(
            (
                (counts_from, counts_ref),
                (order_from, order_ref),
                (obs_from, obs_ref),
                (input_from, input_ref),
            )
        )
    ]
    for copy in copies:
        copy.start()
    blocks, capacity = order_ref.shape
    batches = counts_ref.shape[0]
    per_pair = capacity // batches
    own = lax.axis_index("group")
    lanes = iota((1, capacity), 1)
    batch_ids = iota((batches, capacity), 0)
    earlier = before(capacity)
    row_ids, rank_ids = split(iota((mp * capacity, capacity), 0), per_pair)
    row_slot = split(row_ids, mp)[0] * per_pair + rank_ids

    copies[0].wait()
    start = jnp.int32(0)
    for batch, end in enumerate(span_ends(counts_ref)):
        start = jnp.where(own == batch + 1, end, start)
    count = counts_ref[own]
    filled = lanes < count
    block, shift = split(start, capacity)
    turn = lax.rem(capacity - shift, capacity)
    copies[1].wait()
    first = order_ref[pl.ds(jnp.minimum(block, blocks - 1), 1), :]
    second = order_ref[pl.ds(jnp.minimum(block + 1, blocks - 1), 1), :]
    merged = jnp.where(lanes >= shift, first, second)
    window = pltpu.roll(jnp.broadcast_to(merged, (8, capacity)), turn, 1)[0:1]
    owner, _ = split(window, per_owner)
    by_owner = one_hot((batch_ids == owner) & filled)
    ahead = dot(by_owner, earlier)
    rank = jnp.sum(by_owner.astype(F32) * ahead, axis=0, keepdims=True).astype(I32)
    target = jnp.where(filled, owner * per_pair + rank, -1)
    copies[2].wait()
    send_ref[...] = dot(one_hot(row_slot == target), obs_ref[...]).astype(send_ref.dtype)
    out = pltpu.make_async_copy(send_ref, send_to, sems.at[4])
    out.start()
    slot_ref[0:1, :] = jnp.where(filled, owner, -1)
    slot_ref[1:2, :] = rank
    copies[3].wait()
    out.wait()


def ready_kernel(
    mp, actions, per_owner, counts_from, order_from, value_from, advantage_from, advantage_bias_from,
    hidden_from, cell_from, gate_bias_from, state_from,
    base_ref, to_row_ref, stacked_ref, stacked_bias_ref, hidden_ref, cell_ref, gate_bias_ref, state_ref,
    counts_ref, order_ref, value_ref, advantage_ref, advantage_bias_ref, sems,
):
    pairs = (
        (counts_from, counts_ref),
        (order_from, order_ref),
        (value_from, value_ref),
        (advantage_from, advantage_ref),
        (advantage_bias_from, advantage_bias_ref),
        (hidden_from, hidden_ref),
        (cell_from, cell_ref),
        (gate_bias_from, gate_bias_ref),
        (state_from, state_ref),
    )
    copies = [
        pltpu.make_async_copy(source, held, sems.at[index]) for index, (source, held) in enumerate(pairs)
    ]
    for copy in copies:
        copy.start()
    own = lax.axis_index("group")
    for copy in copies[:5]:
        copy.wait()

    blocks, capacity = order_ref.shape
    batches = counts_ref.shape[0]
    per_pair = capacity // batches
    ends = span_ends(counts_ref)
    lanes = iota((1, capacity), 1)
    batch_ids = iota((batches, capacity), 0)
    earlier = before(capacity)
    actors = iota((per_owner, capacity), 0) + own * per_owner
    carry = jnp.zeros((batches, 1), F32)
    base = jnp.zeros((per_owner, 1), F32)
    for index in range(blocks):
        ids = order_ref[index : index + 1, :]
        here = lanes + index * capacity
        batch = jnp.zeros((1, capacity), I32)
        for end in ends:
            batch = batch + jnp.where(here >= end, 1, 0)
        mine = (ids >= own * per_owner) & (ids < (own + 1) * per_owner)
        by_batch = one_hot((batch_ids == batch) & mine)
        ahead = dot(by_batch, earlier) + carry
        wide = by_batch.astype(F32)
        place = jnp.sum(wide * ahead, axis=0, keepdims=True)
        place = place + (batch * (mp * per_pair)).astype(F32)
        carry = carry + jnp.sum(wide, axis=1, keepdims=True)
        base = base + jnp.sum(jnp.where(ids == actors, place, 0.0), axis=1, keepdims=True)
    base = jnp.broadcast_to(base, base_ref.shape).astype(I32)
    base_ref[...] = base
    owner_rows = to_row_ref.shape[0]
    batch = split(jnp.concatenate([base] * 3, axis=0)[:, 0:1], mp * per_pair)[0]
    row_batch = split(iota((3 * per_owner, owner_rows), 1), mp)[0]
    to_row_ref[...] = jnp.where(row_batch == batch, 1.0, 0.0).T.astype(BF16)

    rows, both = stacked_ref.shape
    width = both // 2
    stride = stride_of(actions)
    row_rank, row_action = split(iota((rows, actions), 0), stride)
    pick = one_hot((row_action == iota((rows, actions), 1)) & (row_rank < per_pair))
    stacked_ref[:, width:] = dot(pick, advantage_ref[...]).astype(BF16)
    row_rank, row_action = split(iota((rows, width), 0), stride)
    value = jnp.broadcast_to(value_ref[...].astype(F32), (rows, width))
    stacked_ref[:, :width] = jnp.where((row_action <= actions) & (row_rank < per_pair), value, 0.0).astype(BF16)
    bias = advantage_bias_ref[...]
    bias = bias - jnp.sum(bias, axis=1, keepdims=True) * (1.0 / actions)
    spread = dot(pieces(jnp.broadcast_to(bias, (8, actions))), pick, ((1,), (1,)))
    stacked_bias_ref[...] = spread[0:1] + spread[8:9] + spread[16:17]
    for copy in copies[5:]:
        copy.wait()


def state_kernel(offsets, hidden_refs, state_ref, bias_ref, gates_ref):
    units = hidden_refs[0].shape[1]
    me = lax.axis_index("mp")
    gates = None
    for ref, offset in zip(hidden_refs, offsets):
        rows = pl.ds(pl.multiple_of(jnp.bitwise_xor(me, offset) * units, units), units)
        term = dot(ref[...], state_ref[rows, :])
        gates = term if gates is None else gates + term
    for k in range(4):
        columns = slice(k * units, (k + 1) * units)
        gates_ref[:, columns] = gates[:, columns] + bias_ref[k : k + 1, :]


def cell_kernel(mp, per_pair, base_ref, rows_ref, gates_ref, cell_ref, input_ref, hidden_ref, next_ref):
    per_owner, units = cell_ref.shape
    features = rows_ref.shape[1]
    base = base_ref[:, 0:1]
    columns = iota((per_owner, rows_ref.shape[0]), 1)
    picks = jnp.concatenate([one_hot(columns == base + part * per_pair) for part in range(mp)], axis=0)
    picked = dot(picks, rows_ref[...]).astype(BF16)
    gates = gates_ref[...]
    for part in range(mp):
        gates = gates + dot(
            picked[part * per_owner : (part + 1) * per_owner],
            input_ref[part * features : (part + 1) * features, :],
        )
    gate = [gates[:, k * units : (k + 1) * units] for k in range(4)]
    cell = jax.nn.sigmoid(gate[1]) * cell_ref[...].astype(F32) + jax.nn.sigmoid(gate[0]) * jnp.tanh(gate[2])
    next_ref[...] = cell.astype(BF16)
    hidden_ref[...] = (jax.nn.sigmoid(gate[3]) * jnp.tanh(cell)).astype(BF16)


def head_kernel(
    mp, per_pair, actions, offsets, base_ref, hidden_refs, cell_ref, head_ref, head_bias_ref,
    to_row_ref, stacked_ref, stacked_bias_ref, value_bias_ref, send_ref, hidden_to, cell_to, sems,
):
    copies = [
        pltpu.make_async_copy(hidden_refs[0], hidden_to, sems.at[0]),
        pltpu.make_async_copy(cell_ref, cell_to, sems.at[1]),
    ]
    for copy in copies:
        copy.start()
    units = head_ref.shape[0] // mp
    me = lax.axis_index("mp")
    total = None
    for ref, offset in zip(hidden_refs, offsets):
        rows = pl.ds(pl.multiple_of(jnp.bitwise_xor(me, offset) * units, units), units)
        term = dot(ref[...], head_ref[rows, :])
        total = term if total is None else total + term
    bias = jnp.concatenate([head_bias_ref[0:1, :], head_bias_ref[1:2, :]], axis=1)
    streams = jnp.maximum(total + bias, 0.0).astype(BF16)
    spread = dot(streams, stacked_ref[...], ((1,), (1,)))
    lanes = iota((1, 128), 1)
    weights = jnp.where(lanes < actions, 1.0 / actions, jnp.where(lanes == actions, -1.0, 0.0))
    mean = jnp.sum(spread[:, :128] * weights, axis=1, keepdims=True)
    spread = spread - mean + (stacked_bias_ref[...] + value_bias_ref[0]) * jnp.where(me == 0, 1.0, 0.0)
    _, rank = split(base_ref[:, 0:1], mp * per_pair)
    lane_rank, lane_action = split(iota((1, spread.shape[1]), 1), stride_of(actions))
    spread = jnp.where((lane_rank == rank) & (lane_action < actions), spread, 0.0)
    out = dot(to_row_ref[...], pieces(spread))
    chunks = out.shape[1] // 128
    for chunk in range(chunks):
        send_ref[pl.ds(chunk, out.shape[0], chunks), 0, :] = out[:, chunk * 128 : (chunk + 1) * 128]
    for copy in copies:
        copy.wait()


def place_kernel(mp, per_pair, slot_ref, rows_ref, out_ref):
    actions, capacity = out_ref.shape
    stride = stride_of(actions)
    chunks = -(-per_pair * stride // 128)
    owners = rows_ref.shape[0] // (mp * chunks)
    owner = slot_ref[0:1, :]
    rank = slot_ref[1:2, :]
    columns = []
    for chunk in range(chunks):
        total = rows_ref[pl.ds(chunk, owners, mp * chunks), 0, :]
        for part in range(1, mp):
            total = total + rows_ref[pl.ds(part * chunks + chunk, owners, mp * chunks), 0, :]
        columns.append(total)
    to_slot = one_hot(iota((owners, capacity), 0) == owner)
    to_slot = jnp.concatenate([to_slot] * 3, axis=0)
    spread = dot(pieces(jnp.concatenate(columns, axis=1)), to_slot, ((0,), (0,)))
    total = jnp.zeros((stride, capacity), F32)
    for index in range(per_pair):
        total = total + jnp.where(rank == index, spread[index * stride : (index + 1) * stride, :], 0.0)
    out_ref[...] = total[:actions, :]


def in_hbm(array):
    return pltpu.with_memory_space_constraint(array, pltpu.HBM)


def call(kernel, out_shape, specs, *args, out_specs=None, scratch=()):
    held = [math.prod(x.shape) * x.dtype.itemsize for x in (*args, *jax.tree.leaves(out_shape))]
    return pl.pallas_call(
        kernel,
        out_shape=out_shape,
        in_specs=specs,
        out_specs=out_specs or jax.tree.map(lambda _: VMEM, out_shape),
        scratch_shapes=list(scratch),
        compiler_params=pltpu.CompilerParams(vmem_limit_bytes=2 * sum(held) + (4 << 20)),
    )(*args)


def gather_parts(part, mp):
    arrays = [part]
    offsets = [0]
    distance = mp // 2
    while distance:
        pairs = [(device, device ^ distance) for device in range(mp)]
        got = []
        for array in arrays:
            got.append(lax.ppermute(array, "mp", pairs))
        arrays += got
        offsets += [offset ^ distance for offset in offsets]
        distance //= 2
    return arrays, offsets


def step(
    observations,
    hidden_state,
    cell_state,
    arrival_order,
    batch_counts,
    input_weight,
    state_weight,
    gate_bias,
    head_weight,
    head_bias,
    value_weight,
    value_bias,
    advantage_weight,
    advantage_bias,
    *,
    mp,
):
    batches = batch_counts.shape[0]
    capacity, features = observations.shape
    per_owner, units = cell_state.shape
    per_pair = capacity // batches
    actions = advantage_weight.shape[1]
    rows = batches * mp
    everyone = ("group", "mp")

    stride = stride_of(actions)
    lanes = -(-per_pair * stride // 128) * 128
    order = arrival_order.reshape(-1, capacity)

    hidden_arrays, offsets = gather_parts(hidden_state, mp)
    send, slot, input_held = call(
        functools.partial(route_kernel, mp, per_owner),
        (
            jax.ShapeDtypeStruct((rows * per_pair, features), BF16),
            jax.ShapeDtypeStruct((2, capacity), I32),
            jax.ShapeDtypeStruct(input_weight.shape, BF16),
        ),
        [HBM, HBM, HBM, HBM],
        *map(in_hbm, (batch_counts, order, observations, input_weight)),
        out_specs=(HBM, VMEM, VMEM),
        scratch=(
            pltpu.SMEM(batch_counts.shape, I32),
            pltpu.VMEM(order.shape, I32),
            pltpu.VMEM(observations.shape, BF16),
            pltpu.VMEM((rows * per_pair, features), BF16),
            pltpu.SemaphoreType.DMA((5,)),
        ),
    )
    got = lax.all_to_all(send, everyone, 0, 0, tiled=True)

    sources = (
        batch_counts,
        order,
        value_weight.T,
        advantage_weight.T,
        advantage_bias.reshape(1, -1),
        hidden_state,
        cell_state,
        gate_bias,
        state_weight,
    )
    base, to_row, stacked, stacked_bias, hidden_held, cell_held, gate_bias_held, state_held = call(
        functools.partial(ready_kernel, mp, actions, per_owner),
        (
            jax.ShapeDtypeStruct((per_owner, 128), I32),
            jax.ShapeDtypeStruct((rows, 3 * per_owner), BF16),
            jax.ShapeDtypeStruct((lanes, 2 * head_bias.shape[1]), BF16),
            jax.ShapeDtypeStruct((1, lanes), F32),
            *(jax.ShapeDtypeStruct(x.shape, x.dtype) for x in sources[5:]),
        ),
        [HBM] * len(sources),
        *map(in_hbm, sources),
        scratch=(
            pltpu.SMEM(batch_counts.shape, I32),
            *(pltpu.VMEM(x.shape, x.dtype) for x in sources[1:5]),
            pltpu.SemaphoreType.DMA((len(sources),)),
        ),
    )
    count = len(hidden_arrays)

    def state_body(*refs):
        state_kernel(offsets, refs[:count], *refs[count:])

    gates = call(
        state_body,
        jax.ShapeDtypeStruct((per_owner, 4 * units), F32),
        [VMEM] * (2 + count),
        hidden_held,
        *hidden_arrays[1:],
        state_held.reshape(state_held.shape[0], -1),
        gate_bias_held,
    )

    state = jax.ShapeDtypeStruct((per_owner, units), BF16)
    next_hidden, next_cell = call(
        functools.partial(cell_kernel, mp, per_pair),
        (state, state),
        [VMEM] * 5,
        base,
        got,
        gates,
        cell_held,
        input_held.reshape(input_held.shape[0], -1),
    )

    next_arrays = [next_hidden]
    next_offsets = [0, *(mp // 2 ^ k for k in range(mp) if k != mp // 2)]
    for offset in next_offsets[1:]:
        pairs = [(device, device ^ offset) for device in range(mp)]
        next_arrays.append(lax.ppermute(next_hidden, "mp", pairs))

    def head_body(base_ref, *refs):
        head_kernel(mp, per_pair, actions, next_offsets, base_ref, refs[:count], *refs[count:])

    values, new_hidden, new_cell = call(
        head_body,
        (jax.ShapeDtypeStruct((rows * lanes // 128, 1, 128), F32), state, state),
        [VMEM] * (7 + count) + [SMEM],
        base,
        *next_arrays,
        next_cell,
        head_weight.reshape(head_weight.shape[0], -1),
        head_bias,
        to_row,
        stacked,
        stacked_bias,
        value_bias,
        out_specs=(VMEM, HBM, HBM),
        scratch=(pltpu.SemaphoreType.DMA((2,)),),
    )
    back = lax.all_to_all(values, everyone, 0, 0, tiled=True)
    placed = call(
        functools.partial(place_kernel, mp, per_pair),
        jax.ShapeDtypeStruct((actions, capacity), F32),
        [VMEM, VMEM],
        slot,
        back,
    )
    return placed.T, new_hidden, new_cell


def solution(mesh):
    placed = (
        P("group", "mp"),
        P("group", "mp"),
        P("group", "mp"),
        P(),
        P(),
        P(None, None, "mp"),
        P(None, None, "mp"),
        P(None, "mp"),
        P(None, None, "mp"),
        P(None, "mp"),
        P("mp", None),
        P(),
        P("mp", None),
        P(),
    )
    return jax.shard_map(
        functools.partial(step, mp=mesh.shape["mp"]),
        mesh=mesh,
        in_specs=placed,
        out_specs=(P("group", None), P("group", "mp"), P("group", "mp")),
        check_vma=False,
    )
```

time: 37.7 us -> 36.9 us (0.979)
  waiting for transfers between devices: 8.2 us -> 4.77 us
  starting transfers between devices: 9.67 us -> 11.4 us
  Pallas kernels: 4.65 us -> 6.1 us
  local copies, waits for them, and re-layouts: 2.08 us -> 0.81 us
  blocking collectives: 11.3 us -> 12.2 us
    ppermute x6 -> x3, waiting for transfers between devices: 6.4 us -> 2.51 us  [gather_parts(): got.append(lax.ppermute(array, 'mp', pairs))]
    ppermute x0 -> x3, starting transfers between devices: none -> 2.21 us  [step(): next_arrays.append(lax.ppermute(next_hidden, 'mp', pairs))]
    ppermute x0 -> x3, waiting for transfers between devices: none -> 1.47 us  [step(): next_arrays.append(lax.ppermute(next_hidden, 'mp', pairs))]
    pallas_call x4 -> x6, Pallas kernels: 4.65 us -> 6.1 us  [call(): pl.pallas_call(kernel, out_shape=out_shape, in_specs=specs, out_specs=out...]
    unnamed x25 -> x7, local copies, waits for them, and re-layouts: 2.08 us -> 0.81 us
    all_to_all x1, waiting for transfers between devices: 1.8 us -> 0.78 us  [step(): got = lax.all_to_all(send, everyone, 0, 0, tiled=True)]
    all_to_all x1, blocking collectives: 11.3 us -> 12.2 us  [step(): back = lax.all_to_all(values, everyone, 0, 0, tiled=True)]
    ppermute x6 -> x3, starting transfers between devices: 2.34 us -> 1.84 us  [gather_parts(): got.append(lax.ppermute(array, 'mp', pairs))]
  transfers between devices with their start and end apart: 7 -> 7, of which waited for: 4 -> 4; matrix products, arithmetic and copies ran while one was open for 5% -> 2% of each run, Pallas kernels for 0% -> 6%
where the time goes in v3:
time: 36.9 us; the launch traced here: 36.6 us
  blocking collectives  12.2 us (33%)
  starting transfers between devices  11.4 us (31%)
  Pallas kernels  6.1 us (17%)
  waiting for transfers between devices  4.77 us (13%)
  between operations  1.38 us (4%)
  local copies, waits for them, and re-layouts  0.81 us (2%)
    all_to_all x1, blocking collectives, step(): back = lax.all_to_all(values, everyone, 0, 0, tiled=True)  12.2 us
    all_to_all x1, starting transfers between devices, step(): got = lax.all_to_all(send, everyone, 0, 0, tiled=True)  7.33 us
    pallas_call x6, Pallas kernels, call(): pl.pallas_call(kernel, out_shape=out_shape, in_specs=specs, out_specs=out...  6.1 us
    ppermute x3, waiting for transfers between devices, gather_parts(): got.append(lax.ppermute(array, 'mp', pairs))  2.51 us
    ppermute x3, starting transfers between devices, step(): next_arrays.append(lax.ppermute(next_hidden, 'mp', pairs))  2.21 us
    ppermute x3, starting transfers between devices, gather_parts(): got.append(lax.ppermute(array, 'mp', pairs))  1.84 us
    ppermute x3, waiting for transfers between devices, step(): next_arrays.append(lax.ppermute(next_hidden, 'mp', pairs))  1.47 us
    unnamed x7, local copies, waits for them, and re-layouts  0.81 us
  transfers between devices with their start and end apart: 7, of which 4 were waited for; matrix products, arithmetic and copies ran while one was open for 2% of the time, Pallas kernels for 6%

profile of v3, /device:TPU:0, one launch (start us, length us, event | category | flops | bytes accessed | tf_op | source)
XLA Modules:
  0.0 36.6 jit_solution(3922460288769742359)
XLA Ops:
  0.6 1.8 %shard_map.157 = (bf16[512,128]{1,0:T(8,128)(2,1)}, s32[2,128]{1,0:T(2,128)S(1)}, bf16[512,4,256]{2,1,0:T(4,128)(2,1)S(1)}) custom-call(s32[8]{0:T(128)} %counts_from.3, s32[4,128]{1,0:T(4,128)} %bitcast.23, bf16[128,128]{1,0:T(8,128)(2,1)} %obs_from.1, bf16[512,4,256]{2,1,0:T(4,128)(2,1)} %input_from.1), custom_call_target="tpu_custom_call" | custom-call | tf_op jit(solution)/shard_map/pallas_call | solution.py:289
  2.4 7.3 %all-to-all-start = ((bf16[32,16,128]{2,1,0:T(8,128)(2,1)}), bf16[32,16,128]{2,1,0:T(8,128)(2,1)S(1)}, u32[]{:S(2)}, u32[]{:S(2)}) async-start(bf16[32,16,128]{2,1,0:T(8,128)(2,1)} %bitcast.4), calls=%async_computation | async-start | bytes 262144 | tf_op jit(solution)/shard_map/all_to_all | solution.py:363
  9.7 1.8 %collective-permute-start = (bf16[64,256]{1,0:T(8,128)(2,1)}, bf16[64,256]{1,0:T(8,128)(2,1)S(1)}, u32[]{:S(2)}, u32[]{:S(2)}) collective-permute-start(bf16[64,256]{1,0:T(8,128)(2,1)} %hidden_from.1), channel_id=1, source_target_pairs={{0,2},{1,3},{2,0},{3,1},{4,6},{5,7},{6,4},{7,5},{8,10},{9,11},{10,... | collective-permute-start | bytes 98312 | tf_op jit(solution)/shard_map/ppermute | solution.py:307
  11.6 0.0 collective-permute-start.1
  11.6 2.5 %collective-permute-done.refs_1_ = bf16[64,256]{1,0:T(8,128)(2,1)S(1)} collective-permute-done((bf16[64,256]{1,0:T(8,128)(2,1)}, bf16[64,256]{1,0:T(8,128)(2,1)S(1)}, u32[]{:S(2)}, u32[]{:S(2)}) %collective-permute-start) | collective-permute-done | bytes 32800 | tf_op jit(solution)/shard_map/ppermute | solution.py:307
  14.1 0.0 collective-permute-start.2
  14.1 1.8 %shard_map.158 = (s32[64,128]{1,0:T(8,128)S(1)}, bf16[32,192]{1,0:T(8,128)(2,1)S(1)}, bf16[384,256]{1,0:T(8,128)(2,1)S(1)}, f32[1,384]{1,0:T(1,128)S(1)}, bf16[6...) custom-call(s32[8]{0:T(128)} %counts_from.3, ...), custom_call_target="tpu_custom_call" | custom-call | tf_op jit(solution)/shard_map/pallas_call | solution.py:289
  15.9 0.5 %copy.17 = bf16[128,8,4,256]{3,1,2,0:T(8,128)(2,1)S(1)} copy(bf16[128,8,4,256]{3,2,1,0:T(4,128)(2,1)S(1)} %bitcast.17) | data formatting | bytes 4194304
  16.4 0.2 copy.18
  16.6 0.0 copy-start.1
  16.6 0.0 collective-permute-done.1.refs_2_
  16.6 0.0 collective-permute-done.2.refs_3_
  16.6 0.0 copy-start
  16.7 0.5 %shard_map.159.gates_ref = f32[64,1024]{1,0:T(8,128)S(1)} custom-call(bf16[64,256]{1,0:T(8,128)(2,1)S(1)} %get-tuple-element.22.refs_0_, bf16[64,256]{1,0:T(8,128)(2,1)S(1)} %collective-permute-done.refs_1_, bf16[64,256]{1,0:T(8,128)(2,1)S(1)} %collective-permute-done.1.refs_2_, bf16[64,256]{1,0:T(8,128)(2,1)S(1)} %collective-permute-done.2.refs_3_, ...), custom_call_target="tpu_custom_call" | custom-call | tf_op jit(solution)/shard_map/pallas_call | solution.py:289
  17.2 0.8 %all-to-all-done = bf16[32,16,128]{2,1,0:T(8,128)(2,1)S(1)} async-done(((bf16[32,16,128]{2,1,0:T(8,128)(2,1)}), bf16[32,16,128]{2,1,0:T(8,128)(2,1)S(1)}, u32[]{:S(2)}, u32[]{:S(2)}) %all-to-all-start) | async-done | bytes 131104 | tf_op jit(solution)/shard_map/all_to_all | solution.py:363
  17.9 0.5 %shard_map.160 = (bf16[64,256]{1,0:T(8,128)(2,1)S(1)}, bf16[64,256]{1,0:T(8,128)(2,1)S(1)}) custom-call(s32[64,128]{1,0:T(8,128)S(1)} %get-tuple-element.20.base_ref, bf16[512,128]{1,0:T(8,128)(2,1)S(1)} %bitcast.20, f32[64,1024]{1,0:T(8,128)S(1)} %shard_map.159.gates_ref, bf16[64,256]{1,0:T(8,128)(2,1)S(1)} %get-tuple-element.25.cell_ref, ...), custom_call_target="tpu_custom_call" | custom-call | tf_op jit(solution)/shard_map/pallas_call | solution.py:289
  18.5 1.1 %collective-permute-start.3 = (bf16[64,256]{1,0:T(8,128)(2,1)S(1)}, bf16[64,256]{1,0:T(8,128)(2,1)S(1)}, u32[]{:S(2)}, u32[]{:S(2)}) collective-permute-start(bf16[64,256]{1,0:T(8,128)(2,1)S(1)} %get-tuple-element.27.refs_0_), channel_id=1, source_target_pairs={{0,2},{1,3},{2,0},{3,1},{4,6},{5,7},{6,4},{7,5},{8,10},{9,11},{10,... | collective-permute-start | bytes 98312 | tf_op jit(solution)/shard_map/ppermute | solution.py:424
  19.5 0.6 %collective-permute-start.4 = (bf16[64,256]{1,0:T(8,128)(2,1)S(1)}, bf16[64,256]{1,0:T(8,128)(2,1)S(1)}, u32[]{:S(2)}, u32[]{:S(2)}) collective-permute-start(bf16[64,256]{1,0:T(8,128)(2,1)S(1)} %get-tuple-element.27.refs_0_), channel_id=1, source_target_pairs={{0,3},{1,2},{2,1},{3,0},{4,7},{5,6},{6,5},{7,4},{8,11},{9,10},{10,... | collective-permute-start | bytes 98312 | tf_op jit(solution)/shard_map/ppermute | solution.py:424
  20.1 0.6 %collective-permute-start.5 = (bf16[64,256]{1,0:T(8,128)(2,1)S(1)}, bf16[64,256]{1,0:T(8,128)(2,1)S(1)}, u32[]{:S(2)}, u32[]{:S(2)}) collective-permute-start(bf16[64,256]{1,0:T(8,128)(2,1)S(1)} %get-tuple-element.27.refs_0_), channel_id=1, source_target_pairs={{0,1},{1,0},{2,3},{3,2},{4,5},{5,4},{6,7},{7,6},{8,9},{9,8},{10,11... | collective-permute-start | bytes 98312 | tf_op jit(solution)/shard_map/ppermute | solution.py:424
  20.7 0.0 copy-done.1
  20.7 0.1 copy.21
  21.4 1.0 %collective-permute-done.3.refs_1_ = bf16[64,256]{1,0:T(8,128)(2,1)S(1)} collective-permute-done((bf16[64,256]{1,0:T(8,128)(2,1)S(1)}, bf16[64,256]{1,0:T(8,128)(2,1)S(1)}, u32[]{:S(2)}, u32[]{:S(2)}) %collective-permute-start.3) | collective-permute-done | bytes 32800 | tf_op jit(solution)/shard_map/ppermute | solution.py:424
  22.4 0.4 %collective-permute-done.4.refs_2_ = bf16[64,256]{1,0:T(8,128)(2,1)S(1)} collective-permute-done((bf16[64,256]{1,0:T(8,128)(2,1)S(1)}, bf16[64,256]{1,0:T(8,128)(2,1)S(1)}, u32[]{:S(2)}, u32[]{:S(2)}) %collective-permute-start.4) | collective-permute-done | bytes 32800 | tf_op jit(solution)/shard_map/ppermute | solution.py:424
  22.9 0.0 collective-permute-done.5.refs_3_
  22.9 0.0 copy-done
  22.9 0.7 %shard_map.161 = (f32[96,1,128]{2,1,0:T(1,128)S(1)}, bf16[64,256]{1,0:T(8,128)(2,1)}, bf16[64,256]{1,0:T(8,128)(2,1)}) custom-call(s32[64,128]{1,0:T(8,128)S(1)} %get-tuple-element.20.base_ref, bf16[64,256]{1,0:T(8,128)(2,1)S(1)} %get-tuple-element.27.refs_0_, bf16[64,256]{1,0:T(8,128)(2,1)S(1)} %collective-permute-done.3.refs_1_, ...), custom_call_target="tpu_custom_call" | custom-call | tf_op jit(solution)/shard_map/pallas_call | solution.py:289
  23.6 12.2 %all_to_all.16.rows_ref = f32[96,1,128]{2,1,0:T(1,128)S(1)} all-to-all(f32[96,1,128]{2,1,0:T(1,128)S(1)} %get-tuple-element.32), channel_id=1, replica_groups=mesh['group'=8,'mp'=4] {'group','mp'}, dimensions={0} | all-to-all | bytes 98304 | tf_op jit(solution)/shard_map/all_to_all | solution.py:445
  35.8 0.8 %shard_map.162 = f32[18,128]{1,0:T(8,128)} custom-call(s32[2,128]{1,0:T(2,128)S(1)} %get-tuple-element.19.slot_ref, f32[96,1,128]{2,1,0:T(1,128)S(1)} %all_to_all.16.rows_ref), custom_call_target="tpu_custom_call" | custom-call | tf_op jit(solution)/shard_map/pallas_call | solution.py:289
Async XLA Ops:
  2.4 15.5 %all-to-all-start = ((bf16[32,16,128]{2,1,0:T(8,128)(2,1)}), bf16[32,16,128]{2,1,0:T(8,128)(2,1)S(1)}, u32[]{:S(2)}, u32[]{:S(2)}) async-start(bf16[32,16,128]{2,1,0:T(8,128)(2,1)} %bitcast.4), calls=%async_computation | async-start | bytes 262144 | tf_op jit(solution)/shard_map/all_to_all | solution.py:363
  9.7 4.3 %collective-permute-start = (bf16[64,256]{1,0:T(8,128)(2,1)}, bf16[64,256]{1,0:T(8,128)(2,1)S(1)}, u32[]{:S(2)}, u32[]{:S(2)}) collective-permute-start(bf16[64,256]{1,0:T(8,128)(2,1)} %hidden_from.1), channel_id=1, source_target_pairs={{0,2},{1,3},{2,0},{3,1},{4,6},{5,7},{6,4},{7,5},{8,10},{9,11},{10,... | collective-permute-start | bytes 98312 | tf_op jit(solution)/shard_map/ppermute | solution.py:307
  11.6 5.1 %collective-permute-start.1 = (bf16[64,256]{1,0:T(8,128)(2,1)}, bf16[64,256]{1,0:T(8,128)(2,1)S(1)}, u32[]{:S(2)}, u32[]{:S(2)}) collective-permute-start(bf16[64,256]{1,0:T(8,128)(2,1)} %hidden_from.1), channel_id=1, source_target_pairs={{0,1},{1,0},{2,3},{3,2},{4,5},{5,4},{6,7},{7,6},{8,9},{9,8},{10,11... | collective-permute-start | bytes 98312 | tf_op jit(solution)/shard_map/ppermute | solution.py:307
  14.1 2.6 %collective-permute-start.2 = (bf16[64,256]{1,0:T(8,128)(2,1)S(1)}, bf16[64,256]{1,0:T(8,128)(2,1)S(1)}, u32[]{:S(2)}, u32[]{:S(2)}) collective-permute-start(bf16[64,256]{1,0:T(8,128)(2,1)S(1)} %collective-permute-done.refs_1_), channel_id=1, source_target_pairs={{0,1},{1,0},{2,3},{3,2},{4,5},{5,4},{6,7},{7,6},{8,9},{9,8},{10,11... | collective-permute-start | bytes 98312 | tf_op jit(solution)/shard_map/ppermute | solution.py:307
  16.6 4.1 %copy-start.1 = (bf16[1024,2,128]{2,1,0:T(2,128)(2,1)S(1)}, bf16[1024,2,128]{2,1,0:T(2,128)(2,1)}, u32[]{:S(2)}) copy-start(bf16[1024,2,128]{2,1,0:T(2,128)(2,1)} %param.22) | copy-start | bytes 1572868
  16.6 6.2 %copy-start = (f32[2,128]{1,0:T(2,128)S(1)}, f32[2,128]{1,0:T(2,128)}, u32[]{:S(2)}) copy-start(f32[2,128]{1,0:T(2,128)} %refs_6_.1) | copy-start | bytes 3076
  18.5 4.0 %collective-permute-start.3 = (bf16[64,256]{1,0:T(8,128)(2,1)S(1)}, bf16[64,256]{1,0:T(8,128)(2,1)S(1)}, u32[]{:S(2)}, u32[]{:S(2)}) collective-permute-start(bf16[64,256]{1,0:T(8,128)(2,1)S(1)} %get-tuple-element.27.refs_0_), channel_id=1, source_target_pairs={{0,2},{1,3},{2,0},{3,1},{4,6},{5,7},{6,4},{7,5},{8,10},{9,11},{10,... | collective-permute-start | bytes 98312 | tf_op jit(solution)/shard_map/ppermute | solution.py:424
  19.5 3.3 %collective-permute-start.4 = (bf16[64,256]{1,0:T(8,128)(2,1)S(1)}, bf16[64,256]{1,0:T(8,128)(2,1)S(1)}, u32[]{:S(2)}, u32[]{:S(2)}) collective-permute-start(bf16[64,256]{1,0:T(8,128)(2,1)S(1)} %get-tuple-element.27.refs_0_), channel_id=1, source_target_pairs={{0,3},{1,2},{2,1},{3,0},{4,7},{5,6},{6,5},{7,4},{8,11},{9,10},{10,... | collective-permute-start | bytes 98312 | tf_op jit(solution)/shard_map/ppermute | solution.py:424
  20.1 2.8 %collective-permute-start.5 = (bf16[64,256]{1,0:T(8,128)(2,1)S(1)}, bf16[64,256]{1,0:T(8,128)(2,1)S(1)}, u32[]{:S(2)}, u32[]{:S(2)}) collective-permute-start(bf16[64,256]{1,0:T(8,128)(2,1)S(1)} %get-tuple-element.27.refs_0_), channel_id=1, source_target_pairs={{0,1},{1,0},{2,3},{3,2},{4,5},{5,4},{6,7},{7,6},{8,9},{9,8},{10,11... | collective-permute-start | bytes 98312 | tf_op jit(solution)/shard_map/ppermute | solution.py:424

commit v4 on v3

--- a/solution.py
+++ b/solution.py
@@ -46,7 +46,7 @@
 
 
 def stride_of(actions):
-    return -(-actions // 8) * 8
+    return -(-(actions + 1) // 8) * 8
 
 
 def span_ends(counts_ref):
@@ -63,8 +63,8 @@
 
 
 def route_kernel(
-    mp, per_owner, counts_from, order_from, obs_from, input_from, send_to, slot_ref,
-    input_ref, counts_ref, order_ref, obs_ref, send_ref, sems,
+    mp, per_owner, counts_from, order_from, obs_from, state_from, send_to, slot_ref,
+    state_ref, counts_ref, order_ref, obs_ref, send_ref, sems,
 ):
     copies = [
         pltpu.make_async_copy(source, held, sems.at[index])
@@ -73,7 +73,7 @@
                 (counts_from, counts_ref),
                 (order_from, order_ref),
                 (obs_from, obs_ref),
-                (input_from, input_ref),
+                (state_from, state_ref),
             )
         )
     ]
@@ -119,8 +119,8 @@
 
 def ready_kernel(
     mp, actions, per_owner, counts_from, order_from, value_from, advantage_from, advantage_bias_from,
-    hidden_from, cell_from, gate_bias_from, state_from,
-    base_ref, to_row_ref, stacked_ref, stacked_bias_ref, hidden_ref, cell_ref, gate_bias_ref, state_ref,
+    hidden_from, cell_from, gate_bias_from, input_from,
+    base_ref, picks_ref, to_row_ref, stacked_ref, stacked_bias_ref, hidden_ref, cell_ref, gate_bias_ref, input_ref,
     counts_ref, order_ref, value_ref, advantage_ref, advantage_bias_ref, sems,
 ):
     pairs = (
@@ -132,7 +132,7 @@
         (hidden_from, hidden_ref),
         (cell_from, cell_ref),
         (gate_bias_from, gate_bias_ref),
-        (state_from, state_ref),
+        (input_from, input_ref),
     )
     copies = [
         pltpu.make_async_copy(source, held, sems.at[index]) for index, (source, held) in enumerate(pairs)
@@ -169,6 +169,10 @@
         base = base + jnp.sum(jnp.where(ids == actors, place, 0.0), axis=1, keepdims=True)
     base = jnp.broadcast_to(base, base_ref.shape).astype(I32)
     base_ref[...] = base
+    columns = iota((per_owner, picks_ref.shape[1]), 1)
+    for part in range(mp):
+        mask = columns == base[:, 0:1] + part * per_pair
+        picks_ref[part * per_owner : (part + 1) * per_owner, :] = one_hot(mask)
     owner_rows = to_row_ref.shape[0]
     batch = split(jnp.concatenate([base] * 3, axis=0)[:, 0:1], mp * per_pair)[0]
     row_batch = split(iota((3 * per_owner, owner_rows), 1), mp)[0]
@@ -184,7 +188,6 @@
     value = jnp.broadcast_to(value_ref[...].astype(F32), (rows, width))
     stacked_ref[:, :width] = jnp.where((row_action <= actions) & (row_rank < per_pair), value, 0.0).astype(BF16)
     bias = advantage_bias_ref[...]
-    bias = bias - jnp.sum(bias, axis=1, keepdims=True) * (1.0 / actions)
     spread = dot(pieces(jnp.broadcast_to(bias, (8, actions))), pick, ((1,), (1,)))
     stacked_bias_ref[...] = spread[0:1] + spread[8:9] + spread[16:17]
     for copy in copies[5:]:
@@ -204,13 +207,10 @@
         gates_ref[:, columns] = gates[:, columns] + bias_ref[k : k + 1, :]
 
 
-def cell_kernel(mp, per_pair, base_ref, rows_ref, gates_ref, cell_ref, input_ref, hidden_ref, next_ref):
+def cell_kernel(mp, picks_ref, rows_ref, gates_ref, cell_ref, input_ref, hidden_ref, next_ref):
     per_owner, units = cell_ref.shape
     features = rows_ref.shape[1]
-    base = base_ref[:, 0:1]
-    columns = iota((per_owner, rows_ref.shape[0]), 1)
-    picks = jnp.concatenate([one_hot(columns == base + part * per_pair) for part in range(mp)], axis=0)
-    picked = dot(picks, rows_ref[...]).astype(BF16)
+    picked = dot(picks_ref[...], rows_ref[...]).astype(BF16)
     gates = gates_ref[...]
     for part in range(mp):
         gates = gates + dot(
@@ -243,13 +243,10 @@
     bias = jnp.concatenate([head_bias_ref[0:1, :], head_bias_ref[1:2, :]], axis=1)
     streams = jnp.maximum(total + bias, 0.0).astype(BF16)
     spread = dot(streams, stacked_ref[...], ((1,), (1,)))
-    lanes = iota((1, 128), 1)
-    weights = jnp.where(lanes < actions, 1.0 / actions, jnp.where(lanes == actions, -1.0, 0.0))
-    mean = jnp.sum(spread[:, :128] * weights, axis=1, keepdims=True)
-    spread = spread - mean + (stacked_bias_ref[...] + value_bias_ref[0]) * jnp.where(me == 0, 1.0, 0.0)
+    spread = spread + (stacked_bias_ref[...] + value_bias_ref[0]) * jnp.where(me == 0, 1.0, 0.0)
     _, rank = split(base_ref[:, 0:1], mp * per_pair)
-    lane_rank, lane_action = split(iota((1, spread.shape[1]), 1), stride_of(actions))
-    spread = jnp.where((lane_rank == rank) & (lane_action < actions), spread, 0.0)
+    lane_rank, _ = split(iota((1, spread.shape[1]), 1), stride_of(actions))
+    spread = jnp.where(lane_rank == rank, spread, 0.0)
     out = dot(to_row_ref[...], pieces(spread))
     chunks = out.shape[1] // 128
     for chunk in range(chunks):
@@ -277,6 +274,9 @@
     total = jnp.zeros((stride, capacity), F32)
     for index in range(per_pair):
         total = total + jnp.where(rank == index, spread[index * stride : (index + 1) * stride, :], 0.0)
+    row = iota((stride, capacity), 0)
+    weights = jnp.where(row < actions, 1.0 / actions, jnp.where(row == actions, -1.0, 0.0))
+    total = total - jnp.sum(total * weights, axis=0, keepdims=True)
     out_ref[...] = total[:actions, :]
 
 
@@ -342,15 +342,15 @@
     order = arrival_order.reshape(-1, capacity)
 
     hidden_arrays, offsets = gather_parts(hidden_state, mp)
-    send, slot, input_held = call(
+    send, slot, state_held = call(
         functools.partial(route_kernel, mp, per_owner),
         (
             jax.ShapeDtypeStruct((rows * per_pair, features), BF16),
             jax.ShapeDtypeStruct((2, capacity), I32),
-            jax.ShapeDtypeStruct(input_weight.shape, BF16),
+            jax.ShapeDtypeStruct(state_weight.shape, BF16),
         ),
         [HBM, HBM, HBM, HBM],
-        *map(in_hbm, (batch_counts, order, observations, input_weight)),
+        *map(in_hbm, (batch_counts, order, observations, state_weight)),
         out_specs=(HBM, VMEM, VMEM),
         scratch=(
             pltpu.SMEM(batch_counts.shape, I32),
@@ -371,12 +371,13 @@
         hidden_state,
         cell_state,
         gate_bias,
-        state_weight,
-    )
-    base, to_row, stacked, stacked_bias, hidden_held, cell_held, gate_bias_held, state_held = call(
+        input_weight,
+    )
+    base, picks, to_row, stacked, stacked_bias, hidden_held, cell_held, gate_bias_held, input_held = call(
         functools.partial(ready_kernel, mp, actions, per_owner),
         (
             jax.ShapeDtypeStruct((per_owner, 128), I32),
+            jax.ShapeDtypeStruct((mp * per_owner, rows * per_pair), BF16),
             jax.ShapeDtypeStruct((rows, 3 * per_owner), BF16),
             jax.ShapeDtypeStruct((lanes, 2 * head_bias.shape[1]), BF16),
             jax.ShapeDtypeStruct((1, lanes), F32),
@@ -407,10 +408,10 @@
 
     state = jax.ShapeDtypeStruct((per_owner, units), BF16)
     next_hidden, next_cell = call(
-        functools.partial(cell_kernel, mp, per_pair),
+        functools.partial(cell_kernel, mp),
         (state, state),
         [VMEM] * 5,
-        base,
+        picks,
         got,
         gates,
         cell_held,

time: 36.9 us -> 36.3 us (0.984)
  blocking collectives: 12.2 us -> 11.8 us
    all_to_all x1, waiting for transfers between devices: 0.78 us -> 1.33 us  [step(): got = lax.all_to_all(send, everyone, 0, 0, tiled=True)]
    all_to_all x1, blocking collectives: 12.2 us -> 11.8 us  [step(): back = lax.all_to_all(values, everyone, 0, 0, tiled=True)]
    unnamed x7 -> x9, local copies, waits for them, and re-layouts: 0.81 us -> 0.81 us
  transfers between devices with their start and end apart: 7 -> 7, of which waited for: 4 -> 3; matrix products, arithmetic and copies ran while one was open for 2% -> 2% of each run, Pallas kernels for 6% -> 5%
where the time goes in v4:
time: 36.3 us; the launch traced here: 36.1 us
  blocking collectives  11.8 us (33%)
  starting transfers between devices  11.4 us (31%)
  Pallas kernels  5.82 us (16%)
  waiting for transfers between devices  4.84 us (13%)
  between operations  1.4 us (4%)
  local copies, waits for them, and re-layouts  0.81 us (2%)
    all_to_all x1, blocking collectives, step(): back = lax.all_to_all(values, everyone, 0, 0, tiled=True)  11.8 us
    all_to_all x1, starting transfers between devices, step(): got = lax.all_to_all(send, everyone, 0, 0, tiled=True)  7.34 us
    pallas_call x6, Pallas kernels, call(): pl.pallas_call(kernel, out_shape=out_shape, in_specs=specs, out_specs=out...  5.82 us
    ppermute x3, waiting for transfers between devices, gather_parts(): got.append(lax.ppermute(array, 'mp', pairs))  2.32 us
    ppermute x3, starting transfers between devices, step(): next_arrays.append(lax.ppermute(next_hidden, 'mp', pairs))  2.21 us
    ppermute x3, starting transfers between devices, gather_parts(): got.append(lax.ppermute(array, 'mp', pairs))  1.84 us
    all_to_all x1, waiting for transfers between devices, step(): got = lax.all_to_all(send, everyone, 0, 0, tiled=True)  1.33 us
    ppermute x3, waiting for transfers between devices, step(): next_arrays.append(lax.ppermute(next_hidden, 'mp', pairs))  1.19 us
  transfers between devices with their start and end apart: 7, of which 3 were waited for; matrix products, arithmetic and copies ran while one was open for 2% of the time, Pallas kernels for 5%

profile of v4, /device:TPU:0, one launch (start us, length us, event | category | flops | bytes accessed | tf_op | source)
XLA Modules:
  0.0 36.1 jit_solution(11615571235463135215)
XLA Ops:
  0.6 0.0 copy-start.2
  0.6 1.9 %shard_map.157 = (bf16[512,128]{1,0:T(8,128)(2,1)}, s32[2,128]{1,0:T(2,128)S(1)}, bf16[1024,4,256]{2,1,0:T(4,128)(2,1)S(1)}) custom-call(s32[8]{0:T(128)} %counts_from.3, s32[4,128]{1,0:T(4,128)} %bitcast.23, bf16[128,128]{1,0:T(8,128)(2,1)} %obs_from.1, bf16[1024,4,256]{2,1,0:T(4,128)(2,1)} %state_from.1), custom_call_target="tpu_custom_call" | custom-call | tf_op jit(solution)/shard_map/pallas_call | solution.py:289
  2.5 7.3 %all-to-all-start = ((bf16[32,16,128]{2,1,0:T(8,128)(2,1)}), bf16[32,16,128]{2,1,0:T(8,128)(2,1)S(1)}, u32[]{:S(2)}, u32[]{:S(2)}) async-start(bf16[32,16,128]{2,1,0:T(8,128)(2,1)} %bitcast.4), calls=%async_computation | async-start | bytes 262144 | tf_op jit(solution)/shard_map/all_to_all | solution.py:363
  9.9 0.0 copy-done.2
  9.9 1.8 %collective-permute-start = (bf16[64,256]{1,0:T(8,128)(2,1)S(1)}, bf16[64,256]{1,0:T(8,128)(2,1)S(1)}, u32[]{:S(2)}, u32[]{:S(2)}) collective-permute-start(bf16[64,256]{1,0:T(8,128)(2,1)S(1)} %copy-done.2), channel_id=1, source_target_pairs={{0,2},{1,3},{2,0},{3,1},{4,6},{5,7},{6,4},{7,5},{8,10},{9,11},{10,... | collective-permute-start | bytes 98312 | tf_op jit(solution)/shard_map/ppermute | solution.py:307
  11.7 0.0 collective-permute-start.1
  11.7 2.3 %collective-permute-done.refs_1_ = bf16[64,256]{1,0:T(8,128)(2,1)S(1)} collective-permute-done((bf16[64,256]{1,0:T(8,128)(2,1)S(1)}, bf16[64,256]{1,0:T(8,128)(2,1)S(1)}, u32[]{:S(2)}, u32[]{:S(2)}) %collective-permute-start) | collective-permute-done | bytes 32800 | tf_op jit(solution)/shard_map/ppermute | solution.py:307
  14.0 0.0 collective-permute-start.2
  14.0 0.5 %copy.17 = bf16[128,8,4,256]{3,1,2,0:T(8,128)(2,1)S(1)} copy(bf16[128,8,4,256]{3,2,1,0:T(4,128)(2,1)S(1)} %bitcast.17) | data formatting | bytes 4194304
  14.5 1.4 %shard_map.158 = (s32[64,128]{1,0:T(8,128)S(1)}, bf16[256,512]{1,0:T(8,128)(2,1)S(1)}, bf16[32,192]{1,0:T(8,128)(2,1)S(1)}, bf16[384,256]{1,0:T(8,128)(2,1)S(1)}...) custom-call(s32[8]{0:T(128)} %counts_from.3, ...), custom_call_target="tpu_custom_call" | custom-call | tf_op jit(solution)/shard_map/pallas_call | solution.py:289
  16.0 0.2 copy.18
  16.2 0.0 collective-permute-done.1.refs_2_
  16.2 0.0 collective-permute-done.2.refs_3_
  16.2 0.0 copy-start.1
  16.2 0.0 copy-start
  16.3 0.5 %shard_map.159.gates_ref = f32[64,1024]{1,0:T(8,128)S(1)} custom-call(bf16[64,256]{1,0:T(8,128)(2,1)S(1)} %get-tuple-element.24.refs_0_, bf16[64,256]{1,0:T(8,128)(2,1)S(1)} %collective-permute-done.refs_1_, bf16[64,256]{1,0:T(8,128)(2,1)S(1)} %collective-permute-done.1.refs_2_, bf16[64,256]{1,0:T(8,128)(2,1)S(1)} %collective-permute-done.2.refs_3_, ...), custom_call_target="tpu_custom_call" | custom-call | tf_op jit(solution)/shard_map/pallas_call | solution.py:289
  16.8 1.3 %all-to-all-done = bf16[32,16,128]{2,1,0:T(8,128)(2,1)S(1)} async-done(((bf16[32,16,128]{2,1,0:T(8,128)(2,1)}), bf16[32,16,128]{2,1,0:T(8,128)(2,1)S(1)}, u32[]{:S(2)}, u32[]{:S(2)}) %all-to-all-start) | async-done | bytes 131104 | tf_op jit(solution)/shard_map/all_to_all | solution.py:363
  18.1 0.5 %shard_map.160 = (bf16[64,256]{1,0:T(8,128)(2,1)S(1)}, bf16[64,256]{1,0:T(8,128)(2,1)S(1)}) custom-call(bf16[256,512]{1,0:T(8,128)(2,1)S(1)} %get-tuple-element.22.picks_ref, bf16[512,128]{1,0:T(8,128)(2,1)S(1)} %bitcast.20, f32[64,1024]{1,0:T(8,128)S(1)} %shard_map.159.gates_ref, bf16[64,256]{1,0:T(8,128)(2,1)S(1)} %get-tuple-element.27.cell_ref, ...), custom_call_target="tpu_custom_call" | custom-call | tf_op jit(solution)/shard_map/pallas_call | solution.py:289
  18.5 0.4 %collective-permute-start.3 = (bf16[64,256]{1,0:T(8,128)(2,1)S(1)}, bf16[64,256]{1,0:T(8,128)(2,1)S(1)}, u32[]{:S(2)}, u32[]{:S(2)}) collective-permute-start(bf16[64,256]{1,0:T(8,128)(2,1)S(1)} %get-tuple-element.29.refs_0_), channel_id=1, source_target_pairs={{0,2},{1,3},{2,0},{3,1},{4,6},{5,7},{6,4},{7,5},{8,10},{9,11},{10,... | collective-permute-start | bytes 98312 | tf_op jit(solution)/shard_map/ppermute | solution.py:425
  19.0 1.2 %collective-permute-start.4 = (bf16[64,256]{1,0:T(8,128)(2,1)S(1)}, bf16[64,256]{1,0:T(8,128)(2,1)S(1)}, u32[]{:S(2)}, u32[]{:S(2)}) collective-permute-start(bf16[64,256]{1,0:T(8,128)(2,1)S(1)} %get-tuple-element.29.refs_0_), channel_id=1, source_target_pairs={{0,3},{1,2},{2,1},{3,0},{4,7},{5,6},{6,5},{7,4},{8,11},{9,10},{10,... | collective-permute-start | bytes 98312 | tf_op jit(solution)/shard_map/ppermute | solution.py:425
  20.2 0.6 %collective-permute-start.5 = (bf16[64,256]{1,0:T(8,128)(2,1)S(1)}, bf16[64,256]{1,0:T(8,128)(2,1)S(1)}, u32[]{:S(2)}, u32[]{:S(2)}) collective-permute-start(bf16[64,256]{1,0:T(8,128)(2,1)S(1)} %get-tuple-element.29.refs_0_), channel_id=1, source_target_pairs={{0,1},{1,0},{2,3},{3,2},{4,5},{5,4},{6,7},{7,6},{8,9},{9,8},{10,11... | collective-permute-start | bytes 98312 | tf_op jit(solution)/shard_map/ppermute | solution.py:425
  20.7 0.0 copy-done.1
  20.8 0.1 copy.21
  21.5 1.2 %collective-permute-done.3.refs_1_ = bf16[64,256]{1,0:T(8,128)(2,1)S(1)} collective-permute-done((bf16[64,256]{1,0:T(8,128)(2,1)S(1)}, bf16[64,256]{1,0:T(8,128)(2,1)S(1)}, u32[]{:S(2)}, u32[]{:S(2)}) %collective-permute-start.3) | collective-permute-done | bytes 32800 | tf_op jit(solution)/shard_map/ppermute | solution.py:425
  22.7 0.0 collective-permute-done.4.refs_2_
  22.7 0.0 collective-permute-done.5.refs_3_
  22.7 0.0 copy-done
  22.7 0.7 %shard_map.161 = (f32[96,1,128]{2,1,0:T(1,128)S(1)}, bf16[64,256]{1,0:T(8,128)(2,1)}, bf16[64,256]{1,0:T(8,128)(2,1)}) custom-call(s32[64,128]{1,0:T(8,128)S(1)} %get-tuple-element.21.base_ref, bf16[64,256]{1,0:T(8,128)(2,1)S(1)} %get-tuple-element.29.refs_0_, bf16[64,256]{1,0:T(8,128)(2,1)S(1)} %collective-permute-done.3.refs_1_, ...), custom_call_target="tpu_custom_call" | custom-call | tf_op jit(solution)/shard_map/pallas_call | solution.py:289
  23.4 11.8 %all_to_all.16.rows_ref = f32[96,1,128]{2,1,0:T(1,128)S(1)} all-to-all(f32[96,1,128]{2,1,0:T(1,128)S(1)} %get-tuple-element.34), channel_id=1, replica_groups=mesh['group'=8,'mp'=4] {'group','mp'}, dimensions={0} | all-to-all | bytes 98304 | tf_op jit(solution)/shard_map/all_to_all | solution.py:446
  35.2 0.8 %shard_map.162 = f32[18,128]{1,0:T(8,128)} custom-call(s32[2,128]{1,0:T(2,128)S(1)} %get-tuple-element.20.slot_ref, f32[96,1,128]{2,1,0:T(1,128)S(1)} %all_to_all.16.rows_ref), custom_call_target="tpu_custom_call" | custom-call | tf_op jit(solution)/shard_map/pallas_call | solution.py:289
Async XLA Ops:
  0.6 9.3 %copy-start.2 = (bf16[64,256]{1,0:T(8,128)(2,1)S(1)}, bf16[64,256]{1,0:T(8,128)(2,1)}, u32[]{:S(2)}) copy-start(bf16[64,256]{1,0:T(8,128)(2,1)} %hidden_from.1) | copy-start | bytes 98308
  2.5 15.5 %all-to-all-start = ((bf16[32,16,128]{2,1,0:T(8,128)(2,1)}), bf16[32,16,128]{2,1,0:T(8,128)(2,1)S(1)}, u32[]{:S(2)}, u32[]{:S(2)}) async-start(bf16[32,16,128]{2,1,0:T(8,128)(2,1)} %bitcast.4), calls=%async_computation | async-start | bytes 262144 | tf_op jit(solution)/shard_map/all_to_all | solution.py:363
  9.9 4.2 %collective-permute-start = (bf16[64,256]{1,0:T(8,128)(2,1)S(1)}, bf16[64,256]{1,0:T(8,128)(2,1)S(1)}, u32[]{:S(2)}, u32[]{:S(2)}) collective-permute-start(bf16[64,256]{1,0:T(8,128)(2,1)S(1)} %copy-done.2), channel_id=1, source_target_pairs={{0,2},{1,3},{2,0},{3,1},{4,6},{5,7},{6,4},{7,5},{8,10},{9,11},{10,... | collective-permute-start | bytes 98312 | tf_op jit(solution)/shard_map/ppermute | solution.py:307
  11.7 4.5 %collective-permute-start.1 = (bf16[64,256]{1,0:T(8,128)(2,1)S(1)}, bf16[64,256]{1,0:T(8,128)(2,1)S(1)}, u32[]{:S(2)}, u32[]{:S(2)}) collective-permute-start(bf16[64,256]{1,0:T(8,128)(2,1)S(1)} %copy-done.2), channel_id=1, source_target_pairs={{0,1},{1,0},{2,3},{3,2},{4,5},{5,4},{6,7},{7,6},{8,9},{9,8},{10,11... | collective-permute-start | bytes 98312 | tf_op jit(solution)/shard_map/ppermute | solution.py:307
  14.0 2.2 %collective-permute-start.2 = (bf16[64,256]{1,0:T(8,128)(2,1)S(1)}, bf16[64,256]{1,0:T(8,128)(2,1)S(1)}, u32[]{:S(2)}, u32[]{:S(2)}) collective-permute-start(bf16[64,256]{1,0:T(8,128)(2,1)S(1)} %collective-permute-done.refs_1_), channel_id=1, source_target_pairs={{0,1},{1,0},{2,3},{3,2},{4,5},{5,4},{6,7},{7,6},{8,9},{9,8},{10,11... | collective-permute-start | bytes 98312 | tf_op jit(solution)/shard_map/ppermute | solution.py:307
  16.2 4.5 %copy-start.1 = (bf16[1024,2,128]{2,1,0:T(2,128)(2,1)S(1)}, bf16[1024,2,128]{2,1,0:T(2,128)(2,1)}, u32[]{:S(2)}) copy-start(bf16[1024,2,128]{2,1,0:T(2,128)(2,1)} %param.22) | copy-start | bytes 1572868
  16.2 6.4 %copy-start = (f32[2,128]{1,0:T(2,128)S(1)}, f32[2,128]{1,0:T(2,128)}, u32[]{:S(2)}) copy-start(f32[2,128]{1,0:T(2,128)} %refs_6_.1) | copy-start | bytes 3076
  18.5 4.1 %collective-permute-start.3 = (bf16[64,256]{1,0:T(8,128)(2,1)S(1)}, bf16[64,256]{1,0:T(8,128)(2,1)S(1)}, u32[]{:S(2)}, u32[]{:S(2)}) collective-permute-start(bf16[64,256]{1,0:T(8,128)(2,1)S(1)} %get-tuple-element.29.refs_0_), channel_id=1, source_target_pairs={{0,2},{1,3},{2,0},{3,1},{4,6},{5,7},{6,4},{7,5},{8,10},{9,11},{10,... | collective-permute-start | bytes 98312 | tf_op jit(solution)/shard_map/ppermute | solution.py:425
  19.0 3.7 %collective-permute-start.4 = (bf16[64,256]{1,0:T(8,128)(2,1)S(1)}, bf16[64,256]{1,0:T(8,128)(2,1)S(1)}, u32[]{:S(2)}, u32[]{:S(2)}) collective-permute-start(bf16[64,256]{1,0:T(8,128)(2,1)S(1)} %get-tuple-element.29.refs_0_), channel_id=1, source_target_pairs={{0,3},{1,2},{2,1},{3,0},{4,7},{5,6},{6,5},{7,4},{8,11},{9,10},{10,... | collective-permute-start | bytes 98312 | tf_op jit(solution)/shard_map/ppermute | solution.py:425
  20.2 2.5 %collective-permute-start.5 = (bf16[64,256]{1,0:T(8,128)(2,1)S(1)}, bf16[64,256]{1,0:T(8,128)(2,1)S(1)}, u32[]{:S(2)}, u32[]{:S(2)}) collective-permute-start(bf16[64,256]{1,0:T(8,128)(2,1)S(1)} %get-tuple-element.29.refs_0_), channel_id=1, source_target_pairs={{0,1},{1,0},{2,3},{3,2},{4,5},{5,4},{6,7},{7,6},{8,9},{9,8},{10,11... | collective-permute-start | bytes 98312 | tf_op jit(solution)/shard_map/ppermute | solution.py:425

commit v5 on v4

--- a/solution.py
+++ b/solution.py
@@ -223,27 +223,43 @@
     hidden_ref[...] = (jax.nn.sigmoid(gate[3]) * jnp.tanh(cell)).astype(BF16)
 
 
-def head_kernel(
-    mp, per_pair, actions, offsets, base_ref, hidden_refs, cell_ref, head_ref, head_bias_ref,
-    to_row_ref, stacked_ref, stacked_bias_ref, value_bias_ref, send_ref, hidden_to, cell_to, sems,
-):
+def head_products(offsets, hidden_refs, head_ref):
+    units = hidden_refs[0].shape[1]
+    me = lax.axis_index("mp")
+    total = None
+    for ref, offset in zip(hidden_refs, offsets):
+        rows = pl.ds(pl.multiple_of(jnp.bitwise_xor(me, offset) * units, units), units)
+        term = dot(ref[...], head_ref[rows, :])
+        total = term if total is None else total + term
+    return total
+
+
+def early_kernel(offsets, hidden_refs, cell_ref, head_ref, head_bias_ref, total_ref, hidden_to, cell_to, sems):
     copies = [
         pltpu.make_async_copy(hidden_refs[0], hidden_to, sems.at[0]),
         pltpu.make_async_copy(cell_ref, cell_to, sems.at[1]),
     ]
     for copy in copies:
         copy.start()
-    units = head_ref.shape[0] // mp
-    me = lax.axis_index("mp")
-    total = None
-    for ref, offset in zip(hidden_refs, offsets):
-        rows = pl.ds(pl.multiple_of(jnp.bitwise_xor(me, offset) * units, units), units)
-        term = dot(ref[...], head_ref[rows, :])
-        total = term if total is None else total + term
     bias = jnp.concatenate([head_bias_ref[0:1, :], head_bias_ref[1:2, :]], axis=1)
-    streams = jnp.maximum(total + bias, 0.0).astype(BF16)
+    total_ref[...] = head_products(offsets, hidden_refs, head_ref) + bias
+    for copy in copies:
+        copy.wait()
+
+
+def middle_kernel(offsets, hidden_refs, head_ref, from_ref, total_ref):
+    total_ref[...] = from_ref[...] + head_products(offsets, hidden_refs, head_ref)
+
+
+def head_kernel(
+    mp, per_pair, actions, offsets, base_ref, total_ref, hidden_refs, head_ref, to_row_ref, stacked_ref,
+    stacked_bias_ref, value_bias_ref, send_ref,
+):
+    total = total_ref[...] + head_products(offsets, hidden_refs, head_ref)
+    streams = jnp.maximum(total, 0.0).astype(BF16)
     spread = dot(streams, stacked_ref[...], ((1,), (1,)))
-    spread = spread + (stacked_bias_ref[...] + value_bias_ref[0]) * jnp.where(me == 0, 1.0, 0.0)
+    first = jnp.where(lax.axis_index("mp") == 0, 1.0, 0.0)
+    spread = spread + (stacked_bias_ref[...] + value_bias_ref[0]) * first
     _, rank = split(base_ref[:, 0:1], mp * per_pair)
     lane_rank, _ = split(iota((1, spread.shape[1]), 1), stride_of(actions))
     spread = jnp.where(lane_rank == rank, spread, 0.0)
@@ -251,8 +267,6 @@
     chunks = out.shape[1] // 128
     for chunk in range(chunks):
         send_ref[pl.ds(chunk, out.shape[0], chunks), 0, :] = out[:, chunk * 128 : (chunk + 1) * 128]
-    for copy in copies:
-        copy.wait()
 
 
 def place_kernel(mp, per_pair, slot_ref, rows_ref, out_ref):
@@ -419,29 +433,59 @@
     )
 
     next_arrays = [next_hidden]
-    next_offsets = [0, *(mp // 2 ^ k for k in range(mp) if k != mp // 2)]
+    next_offsets = list(range(mp))
     for offset in next_offsets[1:]:
         pairs = [(device, device ^ offset) for device in range(mp)]
         next_arrays.append(lax.ppermute(next_hidden, "mp", pairs))
 
-    def head_body(base_ref, *refs):
-        head_kernel(mp, per_pair, actions, next_offsets, base_ref, refs[:count], *refs[count:])
-
-    values, new_hidden, new_cell = call(
+    early = mp // 2
+    head = head_weight.reshape(head_weight.shape[0], -1)
+
+    def early_body(*refs):
+        early_kernel(next_offsets[:early], refs[:early], *refs[early:])
+
+    total, new_hidden, new_cell = call(
+        early_body,
+        (jax.ShapeDtypeStruct((per_owner, head.shape[1]), F32), state, state),
+        [VMEM] * (3 + early),
+        *next_arrays[:early],
+        next_cell,
+        head,
+        head_bias,
+        out_specs=(VMEM, HBM, HBM),
+        scratch=(pltpu.SemaphoreType.DMA((2,)),),
+    )
+    late = len(next_arrays) - 1
+
+    def middle_body(*refs):
+        middle_kernel(next_offsets[early:late], refs[: late - early], *refs[late - early :])
+
+    total = call(
+        middle_body,
+        jax.ShapeDtypeStruct(total.shape, F32),
+        [VMEM] * (2 + late - early),
+        *next_arrays[early:late],
+        head,
+        total,
+    )
+
+    def head_body(base_ref, total_ref, *refs):
+        head_kernel(
+            mp, per_pair, actions, next_offsets[late:], base_ref, total_ref, refs[:1], *refs[1:]
+        )
+
+    values = call(
         head_body,
-        (jax.ShapeDtypeStruct((rows * lanes // 128, 1, 128), F32), state, state),
-        [VMEM] * (7 + count) + [SMEM],
+        jax.ShapeDtypeStruct((rows * lanes // 128, 1, 128), F32),
+        [VMEM] * 7 + [SMEM],
         base,
-        *next_arrays,
-        next_cell,
-        head_weight.reshape(head_weight.shape[0], -1),
-        head_bias,
+        total,
+        next_arrays[late],
+        head,
         to_row,
         stacked,
         stacked_bias,
         value_bias,
-        out_specs=(VMEM, HBM, HBM),
-        scratch=(pltpu.SemaphoreType.DMA((2,)),),
     )
     back = lax.all_to_all(values, everyone, 0, 0, tiled=True)
     placed = call(

time: 36.3 us -> 36.9 us (1.017)
  Pallas kernels: 5.82 us -> 6.37 us
    pallas_call x6 -> x8, Pallas kernels: 5.82 us -> 6.37 us  [call(): pl.pallas_call(kernel, out_shape=out_shape, in_specs=specs, out_specs=out...]
  transfers between devices with their start and end apart: 7 -> 7, of which waited for: 3 -> 3; matrix products, arithmetic and copies ran while one was open for 2% -> 2% of each run, Pallas kernels for 5% -> 7%
where the time goes in v5:
time: 36.9 us; the launch traced here: 36.6 us
  blocking collectives  12.1 us (33%)
  starting transfers between devices  11.1 us (30%)
  Pallas kernels  6.37 us (17%)
  waiting for transfers between devices  4.79 us (13%)
  between operations  1.42 us (4%)
  local copies, waits for them, and re-layouts  0.81 us (2%)
    all_to_all x1, blocking collectives, step(): back = lax.all_to_all(values, everyone, 0, 0, tiled=True)  12.1 us
    all_to_all x1, starting transfers between devices, step(): got = lax.all_to_all(send, everyone, 0, 0, tiled=True)  7.34 us
    pallas_call x8, Pallas kernels, call(): pl.pallas_call(kernel, out_shape=out_shape, in_specs=specs, out_specs=out...  6.37 us
    ppermute x3, waiting for transfers between devices, gather_parts(): got.append(lax.ppermute(array, 'mp', pairs))  2.32 us
    ppermute x3, starting transfers between devices, step(): next_arrays.append(lax.ppermute(next_hidden, 'mp', pairs))  1.93 us
    ppermute x3, starting transfers between devices, gather_parts(): got.append(lax.ppermute(array, 'mp', pairs))  1.84 us
    all_to_all x1, waiting for transfers between devices, step(): got = lax.all_to_all(send, everyone, 0, 0, tiled=True)  1.33 us
    ppermute x3, waiting for transfers between devices, step(): next_arrays.append(lax.ppermute(next_hidden, 'mp', pairs))  1.14 us
  transfers between devices with their start and end apart: 7, of which 3 were waited for; matrix products, arithmetic and copies ran while one was open for 2% of the time, Pallas kernels for 7%

profile of v5, /device:TPU:0, one launch (start us, length us, event | category | flops | bytes accessed | tf_op | source)
XLA Modules:
  0.0 36.6 jit_solution(13495857960193714865)
XLA Ops:
  0.6 0.0 copy-start.2
  0.6 1.9 %shard_map.157 = (bf16[512,128]{1,0:T(8,128)(2,1)}, s32[2,128]{1,0:T(2,128)S(1)}, bf16[1024,4,256]{2,1,0:T(4,128)(2,1)S(1)}) custom-call(s32[8]{0:T(128)} %counts_from.3, s32[4,128]{1,0:T(4,128)} %bitcast.25, bf16[128,128]{1,0:T(8,128)(2,1)} %obs_from.1, bf16[1024,4,256]{2,1,0:T(4,128)(2,1)} %state_from.1), custom_call_target="tpu_custom_call" | custom-call | tf_op jit(solution)/shard_map/pallas_call | solution.py:303
  2.5 7.3 %all-to-all-start = ((bf16[32,16,128]{2,1,0:T(8,128)(2,1)}), bf16[32,16,128]{2,1,0:T(8,128)(2,1)S(1)}, u32[]{:S(2)}, u32[]{:S(2)}) async-start(bf16[32,16,128]{2,1,0:T(8,128)(2,1)} %bitcast.4), calls=%async_computation | async-start | bytes 262144 | tf_op jit(solution)/shard_map/all_to_all | solution.py:377
  9.9 0.0 copy-done.2
  9.9 1.8 %collective-permute-start = (bf16[64,256]{1,0:T(8,128)(2,1)S(1)}, bf16[64,256]{1,0:T(8,128)(2,1)S(1)}, u32[]{:S(2)}, u32[]{:S(2)}) collective-permute-start(bf16[64,256]{1,0:T(8,128)(2,1)S(1)} %copy-done.2), channel_id=1, source_target_pairs={{0,2},{1,3},{2,0},{3,1},{4,6},{5,7},{6,4},{7,5},{8,10},{9,11},{10,... | collective-permute-start | bytes 98312 | tf_op jit(solution)/shard_map/ppermute | solution.py:321
  11.7 0.0 collective-permute-start.1
  11.7 2.3 %collective-permute-done.refs_1_ = bf16[64,256]{1,0:T(8,128)(2,1)S(1)} collective-permute-done((bf16[64,256]{1,0:T(8,128)(2,1)S(1)}, bf16[64,256]{1,0:T(8,128)(2,1)S(1)}, u32[]{:S(2)}, u32[]{:S(2)}) %collective-permute-start) | collective-permute-done | bytes 32800 | tf_op jit(solution)/shard_map/ppermute | solution.py:321
  14.0 0.0 collective-permute-start.2
  14.0 0.5 %copy.17 = bf16[128,8,4,256]{3,1,2,0:T(8,128)(2,1)S(1)} copy(bf16[128,8,4,256]{3,2,1,0:T(4,128)(2,1)S(1)} %bitcast.20) | data formatting | bytes 4194304
  14.5 1.4 %shard_map.158 = (s32[64,128]{1,0:T(8,128)S(1)}, bf16[256,512]{1,0:T(8,128)(2,1)S(1)}, bf16[32,192]{1,0:T(8,128)(2,1)S(1)}, bf16[384,256]{1,0:T(8,128)(2,1)S(1)}...) custom-call(s32[8]{0:T(128)} %counts_from.3, ...), custom_call_target="tpu_custom_call" | custom-call | tf_op jit(solution)/shard_map/pallas_call | solution.py:303
  16.0 0.2 copy.18
  16.2 0.0 collective-permute-done.1.refs_2_
  16.2 0.0 collective-permute-done.2.refs_3_
  16.2 0.0 copy-start.1
  16.2 0.0 copy-start
  16.3 0.5 %shard_map.159.gates_ref = f32[64,1024]{1,0:T(8,128)S(1)} custom-call(bf16[64,256]{1,0:T(8,128)(2,1)S(1)} %get-tuple-element.24.refs_0_, bf16[64,256]{1,0:T(8,128)(2,1)S(1)} %collective-permute-done.refs_1_, bf16[64,256]{1,0:T(8,128)(2,1)S(1)} %collective-permute-done.1.refs_2_, bf16[64,256]{1,0:T(8,128)(2,1)S(1)} %collective-permute-done.2.refs_3_, ...), custom_call_target="tpu_custom_call" | custom-call | tf_op jit(solution)/shard_map/pallas_call | solution.py:303
  16.8 1.3 %all-to-all-done = bf16[32,16,128]{2,1,0:T(8,128)(2,1)S(1)} async-done(((bf16[32,16,128]{2,1,0:T(8,128)(2,1)}), bf16[32,16,128]{2,1,0:T(8,128)(2,1)S(1)}, u32[]{:S(2)}, u32[]{:S(2)}) %all-to-all-start) | async-done | bytes 131104 | tf_op jit(solution)/shard_map/all_to_all | solution.py:377
  18.1 0.5 %shard_map.160 = (bf16[64,256]{1,0:T(8,128)(2,1)S(1)}, bf16[64,256]{1,0:T(8,128)(2,1)S(1)}) custom-call(bf16[256,512]{1,0:T(8,128)(2,1)S(1)} %get-tuple-element.22.picks_ref, bf16[512,128]{1,0:T(8,128)(2,1)S(1)} %bitcast.22, f32[64,1024]{1,0:T(8,128)S(1)} %shard_map.159.gates_ref, bf16[64,256]{1,0:T(8,128)(2,1)S(1)} %get-tuple-element.27.cell_ref, ...), custom_call_target="tpu_custom_call" | custom-call | tf_op jit(solution)/shard_map/pallas_call | solution.py:303
  18.5 0.3 collective-permute-start.4
  18.8 0.7 %collective-permute-start.3 = (bf16[64,256]{1,0:T(8,128)(2,1)S(1)}, bf16[64,256]{1,0:T(8,128)(2,1)S(1)}, u32[]{:S(2)}, u32[]{:S(2)}) collective-permute-start(bf16[64,256]{1,0:T(8,128)(2,1)S(1)} %get-tuple-element.29.refs_0_), channel_id=1, source_target_pairs={{0,2},{1,3},{2,0},{3,1},{4,6},{5,7},{6,4},{7,5},{8,10},{9,11},{10,... | collective-permute-start | bytes 98312 | tf_op jit(solution)/shard_map/ppermute | solution.py:439
  19.5 1.0 %collective-permute-start.5 = (bf16[64,256]{1,0:T(8,128)(2,1)S(1)}, bf16[64,256]{1,0:T(8,128)(2,1)S(1)}, u32[]{:S(2)}, u32[]{:S(2)}) collective-permute-start(bf16[64,256]{1,0:T(8,128)(2,1)S(1)} %get-tuple-element.29.refs_0_), channel_id=1, source_target_pairs={{0,3},{1,2},{2,1},{3,0},{4,7},{5,6},{6,5},{7,4},{8,11},{9,10},{10,... | collective-permute-start | bytes 98312 | tf_op jit(solution)/shard_map/ppermute | solution.py:439
  20.5 0.0 copy-done.1
  20.5 0.1 copy.21
  21.2 0.0 collective-permute-done.4.refs_1_
  21.2 0.0 copy-done
  21.2 0.7 %shard_map.161 = (f32[64,256]{1,0:T(8,128)S(1)}, bf16[64,256]{1,0:T(8,128)(2,1)}, bf16[64,256]{1,0:T(8,128)(2,1)}) custom-call(bf16[64,256]{1,0:T(8,128)(2,1)S(1)} %get-tuple-element.29.refs_0_, bf16[64,256]{1,0:T(8,128)(2,1)S(1)} %collective-permute-done.4.refs_1_, bf16[64,256]{1,0:T(8,128)(2,1)S(1)} %get-tuple-element.30.refs_2_, ...), custom_call_target="tpu_custom_call" | custom-call | tf_op jit(solution)/shard_map/pallas_call | solution.py:303
  21.9 1.1 %collective-permute-done.3.refs_0_ = bf16[64,256]{1,0:T(8,128)(2,1)S(1)} collective-permute-done((bf16[64,256]{1,0:T(8,128)(2,1)S(1)}, bf16[64,256]{1,0:T(8,128)(2,1)S(1)}, u32[]{:S(2)}, u32[]{:S(2)}) %collective-permute-start.3) | collective-permute-done | bytes 32800 | tf_op jit(solution)/shard_map/ppermute | solution.py:439
  23.0 0.1 shard_map.162.total_ref
  23.1 0.0 collective-permute-done.5.refs_0_
  23.2 0.5 %shard_map.163 = f32[96,1,128]{2,1,0:T(1,128)S(1)} custom-call(s32[64,128]{1,0:T(8,128)S(1)} %get-tuple-element.21.base_ref, f32[64,256]{1,0:T(8,128)S(1)} %shard_map.162.total_ref, bf16[64,256]{1,0:T(8,128)(2,1)S(1)} %collective-permute-done.5.refs_0_, bf16[1024,256]{1,0:T(8,128)(2,1)S(1)} %bitcast.18, bf16[32,192]{1,0:T(8,128)(2,1)S(1)} %get-tuple-element.32.refs_2_, ...), custom_call_target="tpu_custom_call" | custom-call | tf_op jit(solution)/shard_map/pallas_call | solution.py:303
  23.6 12.1 %all_to_all.16.rows_ref = f32[96,1,128]{2,1,0:T(1,128)S(1)} all-to-all(f32[96,1,128]{2,1,0:T(1,128)S(1)} %shard_map.163), channel_id=1, replica_groups=mesh['group'=8,'mp'=4] {'group','mp'}, dimensions={0} | all-to-all | bytes 98304 | tf_op jit(solution)/shard_map/all_to_all | solution.py:490
  35.8 0.8 %shard_map.164 = f32[18,128]{1,0:T(8,128)} custom-call(s32[2,128]{1,0:T(2,128)S(1)} %get-tuple-element.20.slot_ref, f32[96,1,128]{2,1,0:T(1,128)S(1)} %all_to_all.16.rows_ref), custom_call_target="tpu_custom_call" | custom-call | tf_op jit(solution)/shard_map/pallas_call | solution.py:303
Async XLA Ops:
  0.6 9.3 %copy-start.2 = (bf16[64,256]{1,0:T(8,128)(2,1)S(1)}, bf16[64,256]{1,0:T(8,128)(2,1)}, u32[]{:S(2)}) copy-start(bf16[64,256]{1,0:T(8,128)(2,1)} %hidden_from.1) | copy-start | bytes 98308
  2.5 15.5 %all-to-all-start = ((bf16[32,16,128]{2,1,0:T(8,128)(2,1)}), bf16[32,16,128]{2,1,0:T(8,128)(2,1)S(1)}, u32[]{:S(2)}, u32[]{:S(2)}) async-start(bf16[32,16,128]{2,1,0:T(8,128)(2,1)} %bitcast.4), calls=%async_computation | async-start | bytes 262144 | tf_op jit(solution)/shard_map/all_to_all | solution.py:377
  9.9 4.2 %collective-permute-start = (bf16[64,256]{1,0:T(8,128)(2,1)S(1)}, bf16[64,256]{1,0:T(8,128)(2,1)S(1)}, u32[]{:S(2)}, u32[]{:S(2)}) collective-permute-start(bf16[64,256]{1,0:T(8,128)(2,1)S(1)} %copy-done.2), channel_id=1, source_target_pairs={{0,2},{1,3},{2,0},{3,1},{4,6},{5,7},{6,4},{7,5},{8,10},{9,11},{10,... | collective-permute-start | bytes 98312 | tf_op jit(solution)/shard_map/ppermute | solution.py:321
  11.7 4.5 %collective-permute-start.1 = (bf16[64,256]{1,0:T(8,128)(2,1)S(1)}, bf16[64,256]{1,0:T(8,128)(2,1)S(1)}, u32[]{:S(2)}, u32[]{:S(2)}) collective-permute-start(bf16[64,256]{1,0:T(8,128)(2,1)S(1)} %copy-done.2), channel_id=1, source_target_pairs={{0,1},{1,0},{2,3},{3,2},{4,5},{5,4},{6,7},{7,6},{8,9},{9,8},{10,11... | collective-permute-start | bytes 98312 | tf_op jit(solution)/shard_map/ppermute | solution.py:321
  14.0 2.2 %collective-permute-start.2 = (bf16[64,256]{1,0:T(8,128)(2,1)S(1)}, bf16[64,256]{1,0:T(8,128)(2,1)S(1)}, u32[]{:S(2)}, u32[]{:S(2)}) collective-permute-start(bf16[64,256]{1,0:T(8,128)(2,1)S(1)} %collective-permute-done.refs_1_), channel_id=1, source_target_pairs={{0,1},{1,0},{2,3},{3,2},{4,5},{5,4},{6,7},{7,6},{8,9},{9,8},{10,11... | collective-permute-start | bytes 98312 | tf_op jit(solution)/shard_map/ppermute | solution.py:321
  16.2 4.2 %copy-start.1 = (bf16[1024,2,128]{2,1,0:T(2,128)(2,1)S(1)}, bf16[1024,2,128]{2,1,0:T(2,128)(2,1)}, u32[]{:S(2)}) copy-start(bf16[1024,2,128]{2,1,0:T(2,128)(2,1)} %param.22) | copy-start | bytes 1572868
  16.2 5.0 %copy-start = (f32[2,128]{1,0:T(2,128)S(1)}, f32[2,128]{1,0:T(2,128)}, u32[]{:S(2)}) copy-start(f32[2,128]{1,0:T(2,128)} %refs_4_.1) | copy-start | bytes 3076
  18.5 2.7 %collective-permute-start.4 = (bf16[64,256]{1,0:T(8,128)(2,1)S(1)}, bf16[64,256]{1,0:T(8,128)(2,1)S(1)}, u32[]{:S(2)}, u32[]{:S(2)}) collective-permute-start(bf16[64,256]{1,0:T(8,128)(2,1)S(1)} %get-tuple-element.29.refs_0_), channel_id=1, source_target_pairs={{0,1},{1,0},{2,3},{3,2},{4,5},{5,4},{6,7},{7,6},{8,9},{9,8},{10,11... | collective-permute-start | bytes 98312 | tf_op jit(solution)/shard_map/ppermute | solution.py:439
  18.8 4.2 %collective-permute-start.3 = (bf16[64,256]{1,0:T(8,128)(2,1)S(1)}, bf16[64,256]{1,0:T(8,128)(2,1)S(1)}, u32[]{:S(2)}, u32[]{:S(2)}) collective-permute-start(bf16[64,256]{1,0:T(8,128)(2,1)S(1)} %get-tuple-element.29.refs_0_), channel_id=1, source_target_pairs={{0,2},{1,3},{2,0},{3,1},{4,6},{5,7},{6,4},{7,5},{8,10},{9,11},{10,... | collective-permute-start | bytes 98312 | tf_op jit(solution)/shard_map/ppermute | solution.py:439
  19.5 3.7 %collective-permute-start.5 = (bf16[64,256]{1,0:T(8,128)(2,1)S(1)}, bf16[64,256]{1,0:T(8,128)(2,1)S(1)}, u32[]{:S(2)}, u32[]{:S(2)}) collective-permute-start(bf16[64,256]{1,0:T(8,128)(2,1)S(1)} %get-tuple-element.29.refs_0_), channel_id=1, source_target_pairs={{0,3},{1,2},{2,1},{3,0},{4,7},{5,6},{6,5},{7,4},{8,11},{9,10},{10,... | collective-permute-start | bytes 98312 | tf_op jit(solution)/shard_map/ppermute | solution.py:439

commit v6 on v5

--- a/solution.py
+++ b/solution.py
@@ -209,14 +209,9 @@
 
 def cell_kernel(mp, picks_ref, rows_ref, gates_ref, cell_ref, input_ref, hidden_ref, next_ref):
     per_owner, units = cell_ref.shape
-    features = rows_ref.shape[1]
     picked = dot(picks_ref[...], rows_ref[...]).astype(BF16)
-    gates = gates_ref[...]
-    for part in range(mp):
-        gates = gates + dot(
-            picked[part * per_owner : (part + 1) * per_owner],
-            input_ref[part * features : (part + 1) * features, :],
-        )
+    wide = [picked[part * per_owner : (part + 1) * per_owner] for part in range(mp)]
+    gates = gates_ref[...] + dot(jnp.concatenate(wide, axis=1), input_ref[...])
     gate = [gates[:, k * units : (k + 1) * units] for k in range(4)]
     cell = jax.nn.sigmoid(gate[1]) * cell_ref[...].astype(F32) + jax.nn.sigmoid(gate[0]) * jnp.tanh(gate[2])
     next_ref[...] = cell.astype(BF16)

time: 36.9 us -> 36.9 us (level)
  no operation moved by 1% of the time
where the time goes in v6:
time: 36.9 us; the launch traced here: 36.6 us
  blocking collectives  12.1 us (33%)
  starting transfers between devices  11.1 us (30%)
  Pallas kernels  6.37 us (17%)
  waiting for transfers between devices  4.79 us (13%)
  between operations  1.42 us (4%)
  local copies, waits for them, and re-layouts  0.81 us (2%)
    all_to_all x1, blocking collectives, step(): back = lax.all_to_all(values, everyone, 0, 0, tiled=True)  12.1 us
    all_to_all x1, starting transfers between devices, step(): got = lax.all_to_all(send, everyone, 0, 0, tiled=True)  7.34 us
    pallas_call x8, Pallas kernels, call(): pl.pallas_call(kernel, out_shape=out_shape, in_specs=specs, out_specs=out...  6.37 us
    ppermute x3, waiting for transfers between devices, gather_parts(): got.append(lax.ppermute(array, 'mp', pairs))  2.32 us
    ppermute x3, starting transfers between devices, step(): next_arrays.append(lax.ppermute(next_hidden, 'mp', pairs))  1.93 us
    ppermute x3, starting transfers between devices, gather_parts(): got.append(lax.ppermute(array, 'mp', pairs))  1.84 us
    all_to_all x1, waiting for transfers between devices, step(): got = lax.all_to_all(send, everyone, 0, 0, tiled=True)  1.33 us
    ppermute x3, waiting for transfers between devices, step(): next_arrays.append(lax.ppermute(next_hidden, 'mp', pairs))  1.14 us
  transfers between devices with their start and end apart: 7, of which 3 were waited for; matrix products, arithmetic and copies ran while one was open for 2% of the time, Pallas kernels for 7%

profile of v6, /device:TPU:0, one launch (start us, length us, event | category | flops | bytes accessed | tf_op | source)
XLA Modules:
  0.0 36.6 jit_solution(12128096424594878862)
XLA Ops:
  0.6 0.0 copy-start.2
  0.6 1.9 %shard_map.157 = (bf16[512,128]{1,0:T(8,128)(2,1)}, s32[2,128]{1,0:T(2,128)S(1)}, bf16[1024,4,256]{2,1,0:T(4,128)(2,1)S(1)}) custom-call(s32[8]{0:T(128)} %counts_from.3, s32[4,128]{1,0:T(4,128)} %bitcast.25, bf16[128,128]{1,0:T(8,128)(2,1)} %obs_from.1, bf16[1024,4,256]{2,1,0:T(4,128)(2,1)} %state_from.1), custom_call_target="tpu_custom_call" | custom-call | tf_op jit(solution)/shard_map/pallas_call | solution.py:298
  2.5 7.3 %all-to-all-start = ((bf16[32,16,128]{2,1,0:T(8,128)(2,1)}), bf16[32,16,128]{2,1,0:T(8,128)(2,1)S(1)}, u32[]{:S(2)}, u32[]{:S(2)}) async-start(bf16[32,16,128]{2,1,0:T(8,128)(2,1)} %bitcast.4), calls=%async_computation | async-start | bytes 262144 | tf_op jit(solution)/shard_map/all_to_all | solution.py:372
  9.9 0.0 copy-done.2
  9.9 1.8 %collective-permute-start = (bf16[64,256]{1,0:T(8,128)(2,1)S(1)}, bf16[64,256]{1,0:T(8,128)(2,1)S(1)}, u32[]{:S(2)}, u32[]{:S(2)}) collective-permute-start(bf16[64,256]{1,0:T(8,128)(2,1)S(1)} %copy-done.2), channel_id=1, source_target_pairs={{0,2},{1,3},{2,0},{3,1},{4,6},{5,7},{6,4},{7,5},{8,10},{9,11},{10,... | collective-permute-start | bytes 98312 | tf_op jit(solution)/shard_map/ppermute | solution.py:316
  11.7 0.0 collective-permute-start.1
  11.7 2.3 %collective-permute-done.refs_1_ = bf16[64,256]{1,0:T(8,128)(2,1)S(1)} collective-permute-done((bf16[64,256]{1,0:T(8,128)(2,1)S(1)}, bf16[64,256]{1,0:T(8,128)(2,1)S(1)}, u32[]{:S(2)}, u32[]{:S(2)}) %collective-permute-start) | collective-permute-done | bytes 32800 | tf_op jit(solution)/shard_map/ppermute | solution.py:316
  14.0 0.0 collective-permute-start.2
  14.0 0.5 %copy.17 = bf16[128,8,4,256]{3,1,2,0:T(8,128)(2,1)S(1)} copy(bf16[128,8,4,256]{3,2,1,0:T(4,128)(2,1)S(1)} %bitcast.20) | data formatting | bytes 4194304
  14.5 1.4 %shard_map.158 = (s32[64,128]{1,0:T(8,128)S(1)}, bf16[256,512]{1,0:T(8,128)(2,1)S(1)}, bf16[32,192]{1,0:T(8,128)(2,1)S(1)}, bf16[384,256]{1,0:T(8,128)(2,1)S(1)}...) custom-call(s32[8]{0:T(128)} %counts_from.3, ...), custom_call_target="tpu_custom_call" | custom-call | tf_op jit(solution)/shard_map/pallas_call | solution.py:298
  16.0 0.2 copy.18
  16.2 0.0 collective-permute-done.1.refs_2_
  16.2 0.0 collective-permute-done.2.refs_3_
  16.2 0.0 copy-start.1
  16.2 0.0 copy-start
  16.3 0.5 %shard_map.159.gates_ref = f32[64,1024]{1,0:T(8,128)S(1)} custom-call(bf16[64,256]{1,0:T(8,128)(2,1)S(1)} %get-tuple-element.24.refs_0_, bf16[64,256]{1,0:T(8,128)(2,1)S(1)} %collective-permute-done.refs_1_, bf16[64,256]{1,0:T(8,128)(2,1)S(1)} %collective-permute-done.1.refs_2_, bf16[64,256]{1,0:T(8,128)(2,1)S(1)} %collective-permute-done.2.refs_3_, ...), custom_call_target="tpu_custom_call" | custom-call | tf_op jit(solution)/shard_map/pallas_call | solution.py:298
  16.8 1.3 %all-to-all-done = bf16[32,16,128]{2,1,0:T(8,128)(2,1)S(1)} async-done(((bf16[32,16,128]{2,1,0:T(8,128)(2,1)}), bf16[32,16,128]{2,1,0:T(8,128)(2,1)S(1)}, u32[]{:S(2)}, u32[]{:S(2)}) %all-to-all-start) | async-done | bytes 131104 | tf_op jit(solution)/shard_map/all_to_all | solution.py:372
  18.1 0.5 %shard_map.160 = (bf16[64,256]{1,0:T(8,128)(2,1)S(1)}, bf16[64,256]{1,0:T(8,128)(2,1)S(1)}) custom-call(bf16[256,512]{1,0:T(8,128)(2,1)S(1)} %get-tuple-element.22.picks_ref, bf16[512,128]{1,0:T(8,128)(2,1)S(1)} %bitcast.22, f32[64,1024]{1,0:T(8,128)S(1)} %shard_map.159.gates_ref, bf16[64,256]{1,0:T(8,128)(2,1)S(1)} %get-tuple-element.27.cell_ref, ...), custom_call_target="tpu_custom_call" | custom-call | tf_op jit(solution)/shard_map/pallas_call | solution.py:298
  18.5 0.3 collective-permute-start.4
  18.8 0.7 %collective-permute-start.3 = (bf16[64,256]{1,0:T(8,128)(2,1)S(1)}, bf16[64,256]{1,0:T(8,128)(2,1)S(1)}, u32[]{:S(2)}, u32[]{:S(2)}) collective-permute-start(bf16[64,256]{1,0:T(8,128)(2,1)S(1)} %get-tuple-element.29.refs_0_), channel_id=1, source_target_pairs={{0,2},{1,3},{2,0},{3,1},{4,6},{5,7},{6,4},{7,5},{8,10},{9,11},{10,... | collective-permute-start | bytes 98312 | tf_op jit(solution)/shard_map/ppermute | solution.py:434
  19.5 1.0 %collective-permute-start.5 = (bf16[64,256]{1,0:T(8,128)(2,1)S(1)}, bf16[64,256]{1,0:T(8,128)(2,1)S(1)}, u32[]{:S(2)}, u32[]{:S(2)}) collective-permute-start(bf16[64,256]{1,0:T(8,128)(2,1)S(1)} %get-tuple-element.29.refs_0_), channel_id=1, source_target_pairs={{0,3},{1,2},{2,1},{3,0},{4,7},{5,6},{6,5},{7,4},{8,11},{9,10},{10,... | collective-permute-start | bytes 98312 | tf_op jit(solution)/shard_map/ppermute | solution.py:434
  20.5 0.0 copy-done.1
  20.5 0.1 copy.21
  21.2 0.0 collective-permute-done.4.refs_1_
  21.2 0.0 copy-done
  21.2 0.7 %shard_map.161 = (f32[64,256]{1,0:T(8,128)S(1)}, bf16[64,256]{1,0:T(8,128)(2,1)}, bf16[64,256]{1,0:T(8,128)(2,1)}) custom-call(bf16[64,256]{1,0:T(8,128)(2,1)S(1)} %get-tuple-element.29.refs_0_, bf16[64,256]{1,0:T(8,128)(2,1)S(1)} %collective-permute-done.4.refs_1_, bf16[64,256]{1,0:T(8,128)(2,1)S(1)} %get-tuple-element.30.refs_2_, ...), custom_call_target="tpu_custom_call" | custom-call | tf_op jit(solution)/shard_map/pallas_call | solution.py:298
  21.9 1.1 %collective-permute-done.3.refs_0_ = bf16[64,256]{1,0:T(8,128)(2,1)S(1)} collective-permute-done((bf16[64,256]{1,0:T(8,128)(2,1)S(1)}, bf16[64,256]{1,0:T(8,128)(2,1)S(1)}, u32[]{:S(2)}, u32[]{:S(2)}) %collective-permute-start.3) | collective-permute-done | bytes 32800 | tf_op jit(solution)/shard_map/ppermute | solution.py:434
  23.0 0.1 shard_map.162.total_ref
  23.1 0.0 collective-permute-done.5.refs_0_
  23.2 0.5 %shard_map.163 = f32[96,1,128]{2,1,0:T(1,128)S(1)} custom-call(s32[64,128]{1,0:T(8,128)S(1)} %get-tuple-element.21.base_ref, f32[64,256]{1,0:T(8,128)S(1)} %shard_map.162.total_ref, bf16[64,256]{1,0:T(8,128)(2,1)S(1)} %collective-permute-done.5.refs_0_, bf16[1024,256]{1,0:T(8,128)(2,1)S(1)} %bitcast.18, bf16[32,192]{1,0:T(8,128)(2,1)S(1)} %get-tuple-element.32.refs_2_, ...), custom_call_target="tpu_custom_call" | custom-call | tf_op jit(solution)/shard_map/pallas_call | solution.py:298
  23.6 12.1 %all_to_all.16.rows_ref = f32[96,1,128]{2,1,0:T(1,128)S(1)} all-to-all(f32[96,1,128]{2,1,0:T(1,128)S(1)} %shard_map.163), channel_id=1, replica_groups=mesh['group'=8,'mp'=4] {'group','mp'}, dimensions={0} | all-to-all | bytes 98304 | tf_op jit(solution)/shard_map/all_to_all | solution.py:485
  35.8 0.8 %shard_map.164 = f32[18,128]{1,0:T(8,128)} custom-call(s32[2,128]{1,0:T(2,128)S(1)} %get-tuple-element.20.slot_ref, f32[96,1,128]{2,1,0:T(1,128)S(1)} %all_to_all.16.rows_ref), custom_call_target="tpu_custom_call" | custom-call | tf_op jit(solution)/shard_map/pallas_call | solution.py:298
Async XLA Ops:
  0.6 9.3 %copy-start.2 = (bf16[64,256]{1,0:T(8,128)(2,1)S(1)}, bf16[64,256]{1,0:T(8,128)(2,1)}, u32[]{:S(2)}) copy-start(bf16[64,256]{1,0:T(8,128)(2,1)} %hidden_from.1) | copy-start | bytes 98308
  2.5 15.5 %all-to-all-start = ((bf16[32,16,128]{2,1,0:T(8,128)(2,1)}), bf16[32,16,128]{2,1,0:T(8,128)(2,1)S(1)}, u32[]{:S(2)}, u32[]{:S(2)}) async-start(bf16[32,16,128]{2,1,0:T(8,128)(2,1)} %bitcast.4), calls=%async_computation | async-start | bytes 262144 | tf_op jit(solution)/shard_map/all_to_all | solution.py:372
  9.9 4.2 %collective-permute-start = (bf16[64,256]{1,0:T(8,128)(2,1)S(1)}, bf16[64,256]{1,0:T(8,128)(2,1)S(1)}, u32[]{:S(2)}, u32[]{:S(2)}) collective-permute-start(bf16[64,256]{1,0:T(8,128)(2,1)S(1)} %copy-done.2), channel_id=1, source_target_pairs={{0,2},{1,3},{2,0},{3,1},{4,6},{5,7},{6,4},{7,5},{8,10},{9,11},{10,... | collective-permute-start | bytes 98312 | tf_op jit(solution)/shard_map/ppermute | solution.py:316
  11.7 4.5 %collective-permute-start.1 = (bf16[64,256]{1,0:T(8,128)(2,1)S(1)}, bf16[64,256]{1,0:T(8,128)(2,1)S(1)}, u32[]{:S(2)}, u32[]{:S(2)}) collective-permute-start(bf16[64,256]{1,0:T(8,128)(2,1)S(1)} %copy-done.2), channel_id=1, source_target_pairs={{0,1},{1,0},{2,3},{3,2},{4,5},{5,4},{6,7},{7,6},{8,9},{9,8},{10,11... | collective-permute-start | bytes 98312 | tf_op jit(solution)/shard_map/ppermute | solution.py:316
  14.0 2.2 %collective-permute-start.2 = (bf16[64,256]{1,0:T(8,128)(2,1)S(1)}, bf16[64,256]{1,0:T(8,128)(2,1)S(1)}, u32[]{:S(2)}, u32[]{:S(2)}) collective-permute-start(bf16[64,256]{1,0:T(8,128)(2,1)S(1)} %collective-permute-done.refs_1_), channel_id=1, source_target_pairs={{0,1},{1,0},{2,3},{3,2},{4,5},{5,4},{6,7},{7,6},{8,9},{9,8},{10,11... | collective-permute-start | bytes 98312 | tf_op jit(solution)/shard_map/ppermute | solution.py:316
  16.2 4.2 %copy-start.1 = (bf16[1024,2,128]{2,1,0:T(2,128)(2,1)S(1)}, bf16[1024,2,128]{2,1,0:T(2,128)(2,1)}, u32[]{:S(2)}) copy-start(bf16[1024,2,128]{2,1,0:T(2,128)(2,1)} %param.22) | copy-start | bytes 1572868
  16.2 5.0 %copy-start = (f32[2,128]{1,0:T(2,128)S(1)}, f32[2,128]{1,0:T(2,128)}, u32[]{:S(2)}) copy-start(f32[2,128]{1,0:T(2,128)} %refs_4_.1) | copy-start | bytes 3076
  18.5 2.7 %collective-permute-start.4 = (bf16[64,256]{1,0:T(8,128)(2,1)S(1)}, bf16[64,256]{1,0:T(8,128)(2,1)S(1)}, u32[]{:S(2)}, u32[]{:S(2)}) collective-permute-start(bf16[64,256]{1,0:T(8,128)(2,1)S(1)} %get-tuple-element.29.refs_0_), channel_id=1, source_target_pairs={{0,1},{1,0},{2,3},{3,2},{4,5},{5,4},{6,7},{7,6},{8,9},{9,8},{10,11... | collective-permute-start | bytes 98312 | tf_op jit(solution)/shard_map/ppermute | solution.py:434
  18.8 4.2 %collective-permute-start.3 = (bf16[64,256]{1,0:T(8,128)(2,1)S(1)}, bf16[64,256]{1,0:T(8,128)(2,1)S(1)}, u32[]{:S(2)}, u32[]{:S(2)}) collective-permute-start(bf16[64,256]{1,0:T(8,128)(2,1)S(1)} %get-tuple-element.29.refs_0_), channel_id=1, source_target_pairs={{0,2},{1,3},{2,0},{3,1},{4,6},{5,7},{6,4},{7,5},{8,10},{9,11},{10,... | collective-permute-start | bytes 98312 | tf_op jit(solution)/shard_map/ppermute | solution.py:434
  19.5 3.7 %collective-permute-start.5 = (bf16[64,256]{1,0:T(8,128)(2,1)S(1)}, bf16[64,256]{1,0:T(8,128)(2,1)S(1)}, u32[]{:S(2)}, u32[]{:S(2)}) collective-permute-start(bf16[64,256]{1,0:T(8,128)(2,1)S(1)} %get-tuple-element.29.refs_0_), channel_id=1, source_target_pairs={{0,3},{1,2},{2,1},{3,0},{4,7},{5,6},{6,5},{7,4},{8,11},{9,10},{10,... | collective-permute-start | bytes 98312 | tf_op jit(solution)/shard_map/ppermute | solution.py:434
